TPU v7x, 128 devices: a whole 4x4x4 slice. The times are simulated.
128 devices in a mesh: rows: 16 (over z, y), zone: 8 (over x, core).
Axes of the slice: x: 4, y: 4, z: 4, core: 2. Of those that a mesh axis runs over, the one named last changes fastest.
Arguments:
- snapshots: float32 [1048576, 256], P(('rows', 'zone')), may hold values from -6 to 6
- tangent: bfloat16 [1048576, 512], P(('rows', 'zone')), may hold values from -0.25 to 0.25
- pattern: int32 [8192, 4], P(('rows', 'zone')), may hold values from 0 to 259, as said below
- forcing: float32 [1048576], P(('rows', 'zone')), may hold values from -6 to 6
- step_index: int32 [256], replicated, may hold values from 0 to 255, each once
Outputs:
- basis: float32 [1048576, 256], P(('rows', 'zone'))
- coefficients: float32 [3, 256], replicated
- residual: float32 [1048576], P(('rows', 'zone'))
Inputs may be any that keep to these rules, and one draw needn't show every extreme that they name: `pattern`: codes of sources 1 and 3 name one of the last 4 blocks of the neighbour, codes of sources 2 and 4 one of its first 4 blocks. `step_index`: each step index once.
All inputs are finite; a program needn't handle non-finite values.
Results may differ from a plain program's by a relative error of at most 0.0003.
Values sent between devices are 32-bit elements; how exact they have to be, the bound alone decides.
A program may use at most 320 MiB of HBM per device.

v0:
```python
import jax
import jax.numpy as jnp
from jax import lax
from jax.sharding import PartitionSpec as P

HALO = 4
STEPS = 3


step_size = 0.25


def shifted(value, axis, steps):
    count = lax.axis_size(axis)
    pairs = [(source, (source + steps) % count) for source in range(count)]
    return lax.ppermute(value, axis, pairs)


def from_behind(shard, axis, by):
    devices = lax.axis_size(axis)
    pairs = [(i, i + by) for i in range(devices) if 0 <= i + by < devices]
    return lax.ppermute(shard, axis, pairs)


def tangent_product(field_in, tangent, pattern):
    highest = lax.Precision.HIGHEST
    block_count, coupled = pattern.shape
    row_count, snap_count = field_in.shape
    block_rows = row_count // block_count
    edge_rows = HALO * block_rows
    tail_part = field_in[row_count - edge_rows :]
    head_part = field_in[:edge_rows]
    rows_prev = shifted(tail_part, "rows", 1)
    rows_next = shifted(head_part, "rows", -1)
    zone_prev = from_behind(tail_part, "zone", 1)
    zone_next = from_behind(head_part, "zone", -1)
    candidates = jnp.concatenate([field_in, rows_prev, rows_next, zone_prev, zone_next], 0)
    source = pattern // block_count
    block_pick = pattern % block_count
    offset_tail = block_pick - (block_count - HALO)
    index_map = jnp.where(
        source == 0,
        block_pick,
        jnp.where(
            source == 1,
            block_count + offset_tail,
            jnp.where(
                source == 2,
                block_count + HALO + block_pick,
                jnp.where(
                    source == 3,
                    block_count + 2 * HALO + offset_tail,
                    block_count + 3 * HALO + block_pick,
                ),
            ),
        ),
    )
    candidates = candidates.reshape(candidates.shape[0] // block_rows, block_rows, snap_count)
    picked = candidates[index_map]
    tile_blocks = tangent.reshape(block_count, block_rows, coupled, block_rows).astype(jnp.float32)
    product = jnp.einsum("gbec,gecs->gbs", tile_blocks, picked, precision=highest)
    return product.reshape(row_count, snap_count)


def shards(snapshots, tangent, pattern, forcing, step_index):
    highest = lax.Precision.HIGHEST
    row_count, snap_count = snapshots.shape
    inverse_count = 1.0 / (row_count * lax.axis_size("rows") * lax.axis_size("zone"))
    identity = jnp.eye(snap_count, dtype=jnp.float32)
    gram_local = jnp.dot(snapshots.T, snapshots, precision=highest) * inverse_count
    gram_matrix = lax.psum(gram_local, ("rows", "zone"))
    factor_low = jnp.linalg.cholesky(gram_matrix)
    inverse = jax.scipy.linalg.solve_triangular(factor_low, identity, lower=True).T
    basis = jnp.dot(snapshots, inverse, precision=highest)
    tangent_image = tangent_product(basis, tangent, pattern)
    trial_basis = basis + step_size * tangent_image
    normal, project, load_vector = lax.psum(
        (
            jnp.dot(trial_basis.T, trial_basis, precision=highest) * inverse_count,
            jnp.dot(trial_basis.T, basis, precision=highest) * inverse_count,
            jnp.dot(trial_basis.T, forcing, precision=highest) * inverse_count,
        ),
        ("rows", "zone"),
    )
    latest = (step_index == jnp.max(step_index)).astype(jnp.float32)
    coeff_now = jnp.dot(latest, factor_low, precision=highest)
    normal_low = jnp.linalg.cholesky(normal)
    history = []
    coeff_old = coeff_now
    for iteration in range(STEPS):
        coeff_old = coeff_now
        right_side = jnp.dot(project, coeff_now, precision=highest) + step_size * load_vector
        coeff_now = jax.scipy.linalg.cho_solve((normal_low, True), right_side)
        history.append(coeff_now)
    residual = (
        jnp.dot(trial_basis, coeff_now, precision=highest)
        - jnp.dot(basis, coeff_old, precision=highest)
        - step_size * forcing
    )
    return (basis, jnp.stack(history), residual)


def solution(mesh):
    in_specs = (
        P(("rows", "zone"), None),
        P(("rows", "zone"), None),
        P(("rows", "zone"), None),
        P(("rows", "zone")),
        P(),
    )
    out_specs = (P(("rows", "zone"), None), P(), P(("rows", "zone")))
    return jax.shard_map(shards, mesh=mesh, in_specs=in_specs, out_specs=out_specs, check_vma=False)
```

profile of v0, /device:TPU:1, one launch (start us, length us, event | category | flops | bytes accessed | tf_op | source)
XLA Modules:
  0.0 614.8 jit_solution(6928881678304809399)
XLA Ops:
  7.2 19.9 %convolution_multiply_fusion.2 = f32[256,256]{0,1:T(8,128)} fusion(f32[8192,256]{1,0:T(8,128)} %param.8), kind=kOutput, calls=%fused_computation.12 | convolution fusion | flops 6442516480 | bytes 8650752 | tf_op jit(solution)/shard_map/dot_general | solution.py:70
  28.1 144.0 %all-reduce.5.cloned.1.call-done = f32[256,256]{0,1:T(8,128)} async-done(((f32[256,256]{0,1:T(8,128)}), f32[256,256]{0,1:T(8,128)}) %all-reduce.5.cloned.1.call-update) | async-done | bytes 262160 | tf_op jit(solution)/shard_map/psum | solution.py:71
  174.2 11.7 %cholesky.130 = f32[128,128]{1,0:T(8,128)S(1)} custom-call(f32[128,128]{1,0:T(8,128)S(1)} %cholesky.194), custom_call_target="Cholesky" | custom-call | tf_op jit(solution)/shard_map/jit(cholesky)/cholesky | solution.py:72
  185.9 9.8 %custom-call.21 = f32[1,128,128]{1,2,0:T(8,128)S(1)} custom-call(f32[1,128,128]{2,1,0:T(8,128)S(1)} %get-tuple-element.73), custom_call_target="InvertDiagBlocksLowerTriangular" | custom-call | tf_op jit(solution)/shard_map/jit(cholesky)/cholesky | solution.py:72
  196.3 11.7 %cholesky.147 = f32[128,128]{1,0:T(8,128)S(1)} custom-call(f32[128,128]{1,0:T(8,128)S(1)} %convolution_subtract_fusion.2), custom_call_target="Cholesky" | custom-call | tf_op jit(solution)/shard_map/jit(cholesky)/cholesky | solution.py:72
  210.2 4.4 while.7
  211.1 1.4 bitcast_dynamic-update-slice_fusion.4
  213.1 1.4 bitcast_dynamic-update-slice_fusion.4
  214.6 19.7 %custom-call.17 = f32[2,128,128]{1,2,0:T(8,128)S(1)} custom-call(f32[2,128,128]{2,1,0:T(8,128)S(1)} %get-tuple-element.20), custom_call_target="InvertDiagBlocksLowerTriangular" | custom-call | tf_op jit(solution)/shard_map/jit(_solve_triangular)/triangular_solve | solution.py:73
  235.1 11.7 %constant_dynamic-update-slice_fusion.4 = (f32[10240,256]{0,1:T(8,128)}, f32[256,8192]{1,0:T(8,128)S(1)}) fusion(f32[8192,256]{1,0:T(8,128)} %param.8, f32[128,256]{1,0:T(8,128)S(1)} %fusion.33, f32[128,256]{1,0:T(8,128)S(1)} %fusion.27), kind=kOutput, calls=%fused_computation.96 | convolution fusion | flops 6442516480 | bytes 25427968 | tf_op jit(solution)/shard_map/dot_general | solution.py:74
  246.8 3.3 copy-done
  251.9 3.9 collective-permute-start.1
  256.6 4.1 collective-permute-start.2
  260.7 12.5 %reshape.63 = bf16[64,128,4,128]{3,2,1,0:T(4,128)(2,1)} reshape(bf16[8192,512]{1,0:T(8,128)(2,1)} %param.9) | data formatting | bytes 16777216 | tf_op jit(solution)/shard_map/reshape | solution.py:60
  273.3 1.9 collective-permute-start.3
  275.2 9.5 %copy.26 = f32[8192,256]{1,0:T(8,128)} copy(f32[8192,256]{0,1:T(8,128)} %bitcast.247) | data formatting | bytes 16777216
  288.4 11.4 %copy.31 = f32[10240,256]{1,0:T(8,128)} copy(f32[10240,256]{0,1:T(8,128)} %constant_dynamic-update-slice_fusion) | data formatting | bytes 20971520 | tf_op jit(solution)/shard_map/reshape | solution.py:58
  299.8 18.9 %gather_fusion = f32[256,128,256]{2,1,0:T(8,128)} fusion(f32[80,128,256]{2,1,0:T(8,128)} %bitcast.249, s32[1024]{0:T(1024)S(1)} %pad_clamp_fusion), kind=kCustom, calls=%fused_computation | custom fusion | bytes 67109888 | tf_op jit(solution)/shard_map/gather | solution.py:59
  318.7 25.2 %bitcast_multiply_fusion = f32[64,256,128]{1,2,0:T(8,128)} fusion(f32[64,4,128,256]{3,2,1,0:T(8,128)} %bitcast.248, bf16[64,128,4,128]{3,2,1,0:T(4,128)(2,1)} %reshape.63), kind=kOutput, calls=%fused_computation.7 | convolution fusion | flops 12886999040 | bytes 50331648 | tf_op jit(solution)/shard_map/gbec,gecs->gbs/dot_general | solution.py:61
  343.9 8.9 %copy.32 = f32[8192,256]{0,1:T(8,128)} copy(f32[8192,256]{1,0:T(8,128)} %bitcast.250) | data formatting | bytes 16777216 | tf_op jit(solution)/shard_map/mul | solution.py:76
  352.8 13.1 %convolution_multiply_fusion = f32[256,256]{0,1:T(8,128)} fusion(f32[256,8192]{1,0:T(8,128)} %copy-done, f32[8192,256]{0,1:T(8,128)} %copy.32), kind=kOutput, calls=%fused_computation.10 | convolution fusion | flops 6444613632 | bytes 17039360 | tf_op jit(solution)/shard_map/dot_general | solution.py:80
  365.9 12.3 %convolution_multiply_fusion.1 = f32[256,256]{0,1:T(8,128)} fusion(f32[8192,256]{0,1:T(8,128)S(1)} %copy-done.1, f32[256,8192]{1,0:T(8,128)} %copy-done), kind=kOutput, calls=%fused_computation.11 | convolution fusion | flops 6444613632 | bytes 17039360 | tf_op jit(solution)/shard_map/dot_general | solution.py:79
  378.3 10.2 %fusion = f32[1,256]{1,0:T(1,128)S(1)} fusion(f32[8192,1]{0,1:T(1,128)S(1)} %bitcast.251, f32[8192,256]{0,1:T(8,128)} %copy.32, f32[256,8192]{1,0:T(8,128)} %copy-done), kind=kOutput, calls=%fused_computation.5 | convolution fusion | flops 27262976 | bytes 16811008 | tf_op jit(solution)/shard_map/dot_general | solution.py:81
  388.5 62.9 %psum.31 = f32[256]{0:T(256)S(1)} all-reduce(f32[256]{0:T(256)S(1)} %broadcast_multiply_fusion), channel_id=1, replica_groups=mesh['rows'=16,'zone'=8] {'rows','zone'}, use_global_device_ids=true, to_apply=%region_8.10 | all-reduce | flops 256 | bytes 2048 | tf_op jit(solution)/shard_map/psum | solution.py:77
  451.3 68.1 %all-reduce.7.cloned.1.call-done = (f32[256,256]{0,1:T(8,128)}, f32[256,256]{0,1:T(8,128)}) async-done(((f32[256,256]{0,1:T(8,128)}, f32[256,256]{0,1:T(8,128)}), (f32[256,256]{0,1:T(8,128)}, f32[256,256]{0,1:T(8,128)})) %all-reduce.7.cloned.1.call-update) | async-done | bytes 524304 | tf_op jit(solution)/shard_map/psum | solution.py:77
  521.6 11.7 %cholesky.164 = f32[128,128]{1,0:T(8,128)S(1)} custom-call(f32[128,128]{1,0:T(8,128)S(1)} %cholesky.197), custom_call_target="Cholesky" | custom-call | tf_op jit(solution)/shard_map/jit(cholesky)/cholesky | solution.py:87
  533.4 9.8 %custom-call.22 = f32[1,128,128]{1,2,0:T(8,128)S(1)} custom-call(f32[1,128,128]{2,1,0:T(8,128)S(1)} %get-tuple-element.69), custom_call_target="InvertDiagBlocksLowerTriangular" | custom-call | tf_op jit(solution)/shard_map/jit(cholesky)/cholesky | solution.py:87
  543.7 11.7 %cholesky.181 = f32[128,128]{1,0:T(8,128)S(1)} custom-call(f32[128,128]{1,0:T(8,128)S(1)} %convolution_subtract_fusion.1), custom_call_target="Cholesky" | custom-call | tf_op jit(solution)/shard_map/jit(cholesky)/cholesky | solution.py:87
  558.0 4.0 while.8
  562.0 19.9 %custom-call.23 = f32[2,128,128]{1,2,0:T(8,128)S(1)} custom-call(f32[2,128,128]{2,1,0:T(8,128)S(1)} %get-tuple-element.33), custom_call_target="InvertDiagBlocksLowerTriangular" | custom-call | tf_op jit(solution)/shard_map/jit(_cho_solve)/triangular_solve | solution.py:93
  586.7 7.9 %fusion.58 = f32[1,8192]{1,0:T(1,128)S(1)} fusion(f32[256,8192]{1,0:T(8,128)} %copy-done, f32[128,1]{0,1:T(1,128)S(1)} %convolution_bitcast_fusion.8, f32[128,1]{0,1:T(1,128)S(1)} %convolution_bitcast_fusion.6), kind=kOutput, calls=%fused_computation.134 | convolution fusion | flops 25166080 | bytes 8422400 | tf_op jit(solution)/shard_map/dot_general | solution.py:97
  595.9 10.4 %fusion.63 = f32[1,8192]{1,0:T(1,128)S(1)} fusion(f32[128,1]{0,1:T(1,128)S(1)} %convolution_bitcast_fusion.3, f32[128,1]{0,1:T(1,128)S(1)} %convolution_bitcast_fusion.1, f32[8192,256]{0,1:T(8,128)} %copy.32, f32[256,8192]{1,0:T(8,128)} %copy-done), kind=kOutput, calls=%fused_computation.140 | convolution fusion | flops 27263232 | bytes 16811008 | tf_op jit(solution)/shard_map/dot_general | solution.py:96
  (102 shorter events, 28.0 us)
Async XLA Ops:
  7.2 20.3 %copy-start.5 = (s32[64,4]{0,1:T(4,128)S(1)}, s32[64,4]{0,1:T(4,128)}, u32[]{:S(2)}) copy-start(s32[64,4]{0,1:T(4,128)} %param.10) | copy-start | bytes 3076
  7.2 20.3 %copy-start.4 = (s32[256]{0:T(256)S(1)}, s32[256]{0:T(256)}, u32[]{:S(2)}) copy-start(s32[256]{0:T(256)} %param.12) | copy-start | bytes 3076
  7.2 164.9 %all-reduce.5.cloned.1.call-start = ((), (), s32[]{:S(2)}) async-start(), calls=%async_computation | async-start | bytes 524288 | tf_op jit(solution)/shard_map/psum | solution.py:71
  27.2 492.3 %all-reduce.7.cloned.1.call-start = ((), (), s32[]{:S(2)}) async-start(), calls=%async_computation.1 | async-start | bytes 1048576 | tf_op jit(solution)/shard_map/psum | solution.py:77
  246.8 3.3 copy-start
  251.0 33.8 %collective-permute-start = (f32[512,256]{0,1:T(8,128)}, f32[512,256]{0,1:T(8,128)S(1)}, u32[]{:S(2)}, u32[]{:S(2)}) collective-permute-start(f32[512,256]{0,1:T(8,128)} %get-tuple-element.65), channel_id=1, source_target_pairs={{0,8},{8,16},{16,24},{24,32},{32,40},{40,48},{48,56},{56,64},{64,7... | collective-permute-start | bytes 1572872 | tf_op jit(solution)/shard_map/ppermute | solution.py:16
  251.9 33.8 %collective-permute-start.1 = (f32[512,256]{0,1:T(8,128)S(1)}, f32[512,256]{0,1:T(8,128)S(1)}, u32[]{:S(2)}, u32[]{:S(2)}) collective-permute-start(f32[512,256]{0,1:T(8,128)S(1)} %get-tuple-element.64), channel_id=1, source_target_pairs={{0,120},{8,0},{16,8},{24,16},{32,24},{40,32},{48,40},{56,48},{64,5... | collective-permute-start | bytes 1572872 | tf_op jit(solution)/shard_map/ppermute | solution.py:16
  256.6 30.1 %collective-permute-start.2 = (f32[512,256]{0,1:T(8,128)}, f32[512,256]{0,1:T(8,128)S(1)}, u32[]{:S(2)}, u32[]{:S(2)}) collective-permute-start(f32[512,256]{0,1:T(8,128)} %get-tuple-element.65), channel_id=1, source_target_pairs={{0,1},{1,2},{2,3},{3,4},{4,5},{5,6},{6,7},{8,9},{9,10},{10,11},{11... | collective-permute-start | bytes 1572872 | tf_op jit(solution)/shard_map/ppermute | solution.py:22
  273.3 14.2 %collective-permute-start.3 = (f32[512,256]{0,1:T(8,128)S(1)}, f32[512,256]{0,1:T(8,128)S(1)}, u32[]{:S(2)}, u32[]{:S(2)}) collective-permute-start(f32[512,256]{0,1:T(8,128)S(1)} %get-tuple-element.64), channel_id=1, source_target_pairs={{1,0},{2,1},{3,2},{4,3},{5,4},{6,5},{7,6},{9,8},{10,9},{11,10},{12... | collective-permute-start | bytes 1572872 | tf_op jit(solution)/shard_map/ppermute | solution.py:22
  352.8 13.1 %copy-start.1 = (f32[8192,256]{0,1:T(8,128)S(1)}, f32[8192,256]{0,1:T(8,128)}, u32[]{:S(2)}) copy-start(f32[8192,256]{0,1:T(8,128)} %copy.32) | copy-start | bytes 25165828
  365.9 12.3 %copy-start.3 = (f32[8192]{0:T(1024)S(1)}, f32[8192]{0:T(1024)}, u32[]{:S(2)}) copy-start(f32[8192]{0:T(1024)} %param.11) | copy-start | bytes 98308
  519.5 75.1 %copy-start.2 = (f32[256,256]{0,1:T(8,128)S(1)}, f32[256,256]{0,1:T(8,128)}, u32[]{:S(2)}) copy-start(f32[256,256]{0,1:T(8,128)} %get-tuple-element.59) | copy-start | bytes 786436
Sparse Core Ops, SparseCore 0:
  27.3 144.7 all-reduce.4
  378.4 141.0 all-reduce.6
where the time goes:
time: 621 us; the launch traced here: 615 us
  waiting for transfers between devices  212 us (34%)
  matrix products  119 us (19%)
  other arithmetic  113 us (18%)
  local copies, waits for them, and re-layouts  79.5 us (13%)
  blocking collectives  62.9 us (10%)
  between operations  17.5 us (3%)
  starting transfers between devices  11.1 us (2%)
    psum x1, waiting for transfers between devices, shards(): gram_matrix = lax.psum(gram_local, ('rows', 'zone'))  144 us
    psum x1, waiting for transfers between devices, shards(): lax.psum((jnp.dot(trial_basis.T, trial_basis, precision=highest) * invers...  68.1 us
    psum x1, blocking collectives, shards(): lax.psum((jnp.dot(trial_basis.T, trial_basis, precision=highest) * invers...  62.9 us
    another operation x7, other arithmetic, shards(): normal_low = jnp.linalg.cholesky(normal)  34.6 us
    another operation x6, other arithmetic, shards(): factor_low = jnp.linalg.cholesky(gram_matrix)  34 us
    dot_general x1, matrix products, tangent_product(): jnp.einsum('gbec,gecs->gbs', tile_blocks, picked, precision=highest)  25.2 us
    another operation x2, other arithmetic, shards(): coeff_now = jax.scipy.linalg.cho_solve((normal_low, True), right_side)  20 us
    dot_general x1, matrix products, shards(): jnp.dot(snapshots.T, snapshots, precision=highest) * inverse_count  19.9 us
  transfers between devices with their start and end apart: 6, of which 2 were waited for; matrix products, arithmetic and copies ran while one was open for 6% of the time, Pallas kernels for 0%

commit v1 on v0

v1 whole, which is shorter than its diff:
```python
import functools

import jax
import jax.numpy as jnp
from jax import lax
from jax.experimental import pallas as pl
from jax.experimental.pallas import tpu as pltpu
from jax.sharding import PartitionSpec as P

HALO = 4
STEPS = 3
STEP = 0.25
B = 128
N = 256
CHUNK = 1024
PACK = 1536
F32 = jnp.float32
BF16 = jnp.bfloat16
HI = lax.Precision.HIGHEST
MESH = pl.DeviceIdType.MESH


def split(x):
    hi = x.astype(BF16)
    return hi, (x - hi.astype(F32)).astype(BF16)


def tdot(a, b):
    return lax.dot_general(a, b, (((0,), (0,)), ((), ())), preferred_element_type=F32)


def gram_kernel(s_ref, sh_ref, sl_ref, g_ref):
    step = pl.program_id(0)

    @pl.when(step == 0)
    def _():
        g_ref[...] = jnp.zeros_like(g_ref)

    hi, lo = split(s_ref[...])
    sh_ref[...] = hi
    sl_ref[...] = lo
    g_ref[...] += tdot(hi, hi)


def gram(snapshots):
    rows = snapshots.shape[0]
    return pl.pallas_call(
        gram_kernel,
        grid=(rows // CHUNK,),
        in_specs=[pl.BlockSpec((CHUNK, N), lambda i: (i, 0))],
        out_specs=[
            pl.BlockSpec((CHUNK, N), lambda i: (i, 0)),
            pl.BlockSpec((CHUNK, N), lambda i: (i, 0)),
            pl.BlockSpec((N, N), lambda i: (0, 0)),
        ],
        out_shape=[
            jax.ShapeDtypeStruct((rows, N), BF16),
            jax.ShapeDtypeStruct((rows, N), BF16),
            jax.ShapeDtypeStruct((N, N), F32),
        ],
        compiler_params=pltpu.CompilerParams(vmem_limit_bytes=24 << 20),
        cost_estimate=pl.CostEstimate(flops=4 * rows * N * N, bytes_accessed=8 * rows * N, transcendentals=0),
        name="gram",
    )(snapshots)


def image_kernel(
    index_ref, t_ref, f_ref, g_ref, rp_ref, rn_ref, zp_ref, zn_ref, sh_hbm, sl_hbm, y_ref, pack_ref,
    cand_h, cand_l, left, right, acc, load_acc, sem,
):
    step = pl.program_id(0)
    rows = sh_hbm.shape[0]
    edge = HALO * B

    @pl.when(step == 0)
    def _():
        one = pltpu.make_async_copy(sh_hbm, cand_h.at[pl.ds(0, rows)], sem.at[0])
        two = pltpu.make_async_copy(sl_hbm, cand_l.at[pl.ds(0, rows)], sem.at[1])
        one.start()
        two.start()
        for i, ref in enumerate((rp_ref, rn_ref, zp_ref, zn_ref)):
            hi, lo = split(ref[...])
            cand_h[pl.ds(rows + i * edge, edge), :] = hi
            cand_l[pl.ds(rows + i * edge, edge), :] = lo
        acc[...] = jnp.zeros_like(acc)
        load_acc[...] = jnp.zeros_like(load_acc)
        one.wait()
        two.wait()

    groups = CHUNK // B
    force = f_ref[...].T
    total = jnp.zeros((8, N), F32)
    for g in range(groups):
        picks = [pl.ds(pl.multiple_of(index_ref[step * groups + g, e] * B, B), B) for e in range(4)]
        tiles = t_ref[g * B : (g + 1) * B, :]
        image = jnp.dot(tiles, jnp.concatenate([cand_h[p, :] for p in picks], axis=0), preferred_element_type=F32)
        image += jnp.dot(tiles, jnp.concatenate([cand_l[p, :] for p in picks], axis=0), preferred_element_type=F32)
        own = pl.ds(pl.multiple_of(step * CHUNK + g * B, B), B)
        y = cand_h[own, :].astype(F32) + cand_l[own, :].astype(F32) + STEP * image
        y_ref[g * B : (g + 1) * B, :] = y
        hi, lo = split(y)
        left[g * B : (g + 1) * B, :N] = hi
        left[g * B : (g + 1) * B, N : 2 * N] = lo
        right[g * B : (g + 1) * B, N:] = hi
        total += jnp.sum((y * force[:, g : g + 1]).reshape(B // 8, 8, N), axis=0)
    load_acc[...] += total
    here = pl.ds(pl.multiple_of(step * CHUNK, CHUNK), CHUNK)
    left[:, 2 * N :] = cand_l[here, :]
    right[:, :N] = cand_h[here, :]
    both = tdot(left[...], right[...])
    acc[0] += both[:N, :N] + both[N : 2 * N, :N]
    acc[1] += both[:N, N:] * 0.5 + both[N : 2 * N, N:]
    acc[2] += both[2 * N :, N:]
    acc[3] += both[2 * N :, :N]

    @pl.when(step == pl.num_programs(0) - 1)
    def _():
        normal = acc[1] + acc[1].T
        project = acc[0] + acc[2].T
        half = g_ref[...] * 0.5 + acc[3]
        gram_matrix = half + half.T
        blocks = []
        for matrix in (gram_matrix, normal):
            blocks += [matrix[:B, :B], matrix[:B, B:], matrix[B:, B:]]
        blocks += [project[:B, :B], project[:B, B:], project[B:, :B], project[B:, B:]]
        for i, block in enumerate(blocks):
            pack_ref[i * B : (i + 1) * B, :] = block
        load = jnp.sum(load_acc[...], axis=0, keepdims=True)
        pack_ref[10 * B :, :] = jnp.zeros((PACK - 10 * B, B), F32)
        pack_ref[10 * B : 10 * B + 1, :] = load[:, :B]
        pack_ref[10 * B + 1 : 10 * B + 2, :] = load[:, B:]


def image(index_map, tangent, forcing, gram_local, halos, sh, sl):
    rows = sh.shape[0]
    edge = HALO * B
    whole = lambda i, *_: (0, 0)
    return pl.pallas_call(
        image_kernel,
        grid_spec=pltpu.PrefetchScalarGridSpec(
            num_scalar_prefetch=1,
            grid=(rows // CHUNK,),
            in_specs=[
                pl.BlockSpec((CHUNK, 4 * B), lambda i, *_: (i, 0)),
                pl.BlockSpec((CHUNK // B, B), lambda i, *_: (i, 0)),
                pl.BlockSpec((N, N), whole, pipeline_mode=pl.Buffered(1)),
            ]
            + [pl.BlockSpec((edge, N), whole, pipeline_mode=pl.Buffered(1))] * 4
            + [pl.BlockSpec(memory_space=pl.ANY)] * 2,
            out_specs=[
                pl.BlockSpec((CHUNK, N), lambda i, *_: (i, 0)),
                pl.BlockSpec((PACK, B), whole),
            ],
            scratch_shapes=[
                pltpu.VMEM((rows + 4 * edge, N), BF16),
                pltpu.VMEM((rows + 4 * edge, N), BF16),
                pltpu.VMEM((CHUNK, 3 * N), BF16),
                pltpu.VMEM((CHUNK, 2 * N), BF16),
                pltpu.VMEM((4, N, N), F32),
                pltpu.VMEM((8, N), F32),
                pltpu.SemaphoreType.DMA((2,)),
            ],
        ),
        out_shape=[
            jax.ShapeDtypeStruct((rows, N), F32),
            jax.ShapeDtypeStruct((PACK, B), F32),
        ],
        compiler_params=pltpu.CompilerParams(vmem_limit_bytes=40 << 20),
        cost_estimate=pl.CostEstimate(flops=24 * rows * N * N, bytes_accessed=16 * rows * N, transcendentals=0),
        name="image",
    )(index_map, tangent, forcing, gram_local, *halos, sh, sl)


PARTS = 3
PART = PACK // PARTS
STAGE_SLOTS = (1, 3, 3, 3, 3, 3, 1)
STAGE_BASE = tuple(PARTS * sum(STAGE_SLOTS[:i]) for i in range(7))


def reduce_kernel(x_ref, o_ref, acc1, acc2, got0, got1, got2, got3, send_sem, recv_sem):
    rows_id = lax.axis_index("rows")
    zone_id = lax.axis_index("zone")
    core = zone_id % 2
    place = {"x": zone_id // 2, "y": rows_id % 4, "z": rows_id // 4}
    orders = (("x", "y", "z"), ("y", "z", "x"), ("z", "x", "y"))

    def device(axis, shift):
        at = dict(place)
        if axis == "core":
            return (rows_id, at["x"] * 2 + (1 - core))
        at[axis] = (at[axis] + shift) % 4
        return (at["z"] * 4 + at["y"], at["x"] * 2 + core)

    barrier = pltpu.get_barrier_semaphore()
    for axis, shift in [("core", 1)] + [(a, s) for a in "xyz" for s in (1, 2, 3)]:
        pl.semaphore_signal(barrier, inc=1, device_id=device(axis, shift), device_id_type=MESH)
    pl.semaphore_wait(barrier, 10)

    live = {}

    def send(stage, part, slot, src, dst, axis, shift):
        k = STAGE_BASE[stage] + part * STAGE_SLOTS[stage] + slot
        copy = pltpu.make_async_remote_copy(
            src_ref=src, dst_ref=dst, send_sem=send_sem.at[k], recv_sem=recv_sem.at[k],
            device_id=device(axis, shift), device_id_type=MESH,
        )
        copy.start()
        live[stage, part, slot] = copy

    def arrive(stage, part):
        for slot in range(STAGE_SLOTS[stage]):
            live[stage, part, slot].wait_recv()

    half = PART // 2
    quarter = half // 4
    piece = quarter // 4
    mine = core * half
    for p in range(PARTS):
        send(0, p, 0, x_ref.at[pl.ds(p * PART + (1 - core) * half, half)], got0.at[p], "core", 1)
    for p, (a, b, c) in enumerate(orders):
        arrive(0, p)
        acc1[p] = x_ref[pl.ds(p * PART + mine, half), :] + got0[p]
        for o in (1, 2, 3):
            there = (place[a] + o) % 4
            send(1, p, o - 1, acc1.at[p, pl.ds(there * quarter, quarter)], got1.at[p, o - 1], a, o)
    for p, (a, b, c) in enumerate(orders):
        arrive(1, p)
        acc2[p] = acc1[p, pl.ds(place[a] * quarter, quarter), :] + got1[p, 0] + got1[p, 1] + got1[p, 2]
        for o in (1, 2, 3):
            there = (place[b] + o) % 4
            send(2, p, o - 1, acc2.at[p, pl.ds(there * piece, piece)], got2.at[p, o - 1], b, o)
    for p, (a, b, c) in enumerate(orders):
        arrive(2, p)
        got3[p, place[c]] = acc2[p, pl.ds(place[b] * piece, piece), :] + got2[p, 0] + got2[p, 1] + got2[p, 2]
        for o in (1, 2, 3):
            send(3, p, o - 1, got3.at[p, place[c]], got3.at[p, place[c]], c, o)
    for p, (a, b, c) in enumerate(orders):
        arrive(3, p)
        spot = p * PART + mine + place[a] * quarter + place[b] * piece
        o_ref[pl.ds(spot, piece), :] = got3[p, 0] + got3[p, 1] + got3[p, 2] + got3[p, 3]
        for o in (1, 2, 3):
            send(4, p, o - 1, o_ref.at[pl.ds(spot, piece)], o_ref.at[pl.ds(spot, piece)], b, o)
    for p, (a, b, c) in enumerate(orders):
        arrive(4, p)
        spot = p * PART + mine + place[a] * quarter
        for o in (1, 2, 3):
            send(5, p, o - 1, o_ref.at[pl.ds(spot, quarter)], o_ref.at[pl.ds(spot, quarter)], a, o)
    for p in range(PARTS):
        arrive(5, p)
        spot = p * PART + mine
        send(6, p, 0, o_ref.at[pl.ds(spot, half)], o_ref.at[pl.ds(spot, half)], "core", 1)
    for p in range(PARTS):
        arrive(6, p)
    for copy in live.values():
        copy.wait_send()


def reduce_all(pack):
    half = PART // 2
    count = PARTS * sum(STAGE_SLOTS)
    return pl.pallas_call(
        reduce_kernel,
        out_shape=jax.ShapeDtypeStruct((PACK, B), F32),
        in_specs=[pl.BlockSpec(memory_space=pltpu.VMEM)],
        out_specs=pl.BlockSpec(memory_space=pltpu.VMEM),
        scratch_shapes=[
            pltpu.VMEM((PARTS, half, B), F32),
            pltpu.VMEM((PARTS, half // 4, B), F32),
            pltpu.VMEM((PARTS, half, B), F32),
            pltpu.VMEM((PARTS, 3, half // 4, B), F32),
            pltpu.VMEM((PARTS, 3, half // 16, B), F32),
            pltpu.VMEM((PARTS, 4, half // 16, B), F32),
            pltpu.SemaphoreType.DMA((count,)),
            pltpu.SemaphoreType.DMA((count,)),
        ],
        compiler_params=pltpu.CompilerParams(collective_id=0, has_side_effects=True, vmem_limit_bytes=16 << 20),
        name="reduce_all",
    )(pack)


def factor_blocks(matrices):
    tiles = [[m[8 * t : 8 * t + 8, :] for t in range(16)] for m in matrices]
    lane = lax.broadcasted_iota(jnp.int32, (8, B), 1)
    sub = lax.broadcasted_iota(jnp.int32, (8, B), 0)
    inverse = [[(lane == sub + 8 * t).astype(F32) for t in range(16)] for _ in matrices]
    for k in range(B):
        t0, i = divmod(k, 8)
        for a, e in zip(tiles, inverse):
            pivot = lax.rsqrt(a[t0][i : i + 1, k : k + 1])
            row = a[t0][i : i + 1, :] * pivot
            erow = e[t0][i : i + 1, :] * pivot
            for t in range(t0, 16):
                scale = a[t][:, k : k + 1] * pivot
                new_a = a[t] - scale * row
                new_e = e[t] - scale * erow
                if t == t0:
                    new_a = jnp.where(sub > i, new_a, jnp.where(sub == i, row, a[t]))
                    new_e = jnp.where(sub > i, new_e, jnp.where(sub == i, erow, e[t]))
                a[t] = new_a
                e[t] = new_e
    upper = [
        jnp.concatenate([jnp.where(lane >= sub + 8 * t, a[t], 0.0) for t in range(16)], axis=0) for a in tiles
    ]
    return upper, [jnp.concatenate(e, axis=0) for e in inverse]


def dotf(a, b, dims):
    return lax.dot_general(a, b, ((dims[:1], dims[1:]), ((), ())), precision=HI, preferred_element_type=F32)


def split3(x):
    hi = x.astype(BF16)
    rest = x - hi.astype(F32)
    mid = rest.astype(BF16)
    return hi, mid, (rest - mid.astype(F32)).astype(BF16)


def row_dot(a, b, dims):
    left, right = split3(a), split3(b)
    total = jnp.zeros((8, N), F32)
    for i, j in ((2, 0), (1, 1), (0, 2), (1, 0), (0, 1), (0, 0)):
        total += lax.dot_general(
            left[i], right[j], ((dims[:1], dims[1:]), ((), ())), preferred_element_type=F32
        )
    return total


def solve_kernel(x_ref, step_ref, wh_ref, wl_ref, d_ref, c_ref, now):
    scale = 1.0 / (8192 * 128)
    block = lambda i: x_ref[i * B : (i + 1) * B, :] * scale
    g11, g12, g22, n11, n12, n22 = (block(i) for i in range(6))
    (u_g, u_n), (e_g, e_n) = factor_blocks([g11, n11])
    u12_g = dotf(e_g, g12, (1, 0))
    u12_n = dotf(e_n, n12, (1, 0))
    s_g = g22 - dotf(u12_g, u12_g, (0, 0))
    s_n = n22 - dotf(u12_n, u12_n, (0, 0))
    (v_g, v_n), (h_g, h_n) = factor_blocks([s_g, s_n])
    low_g = -dotf(h_g, dotf(u12_g, e_g, (0, 0)), (1, 0))
    low_n = -dotf(h_n, dotf(u12_n, e_n, (0, 0)), (1, 0))
    zero = jnp.zeros((B, B), F32)
    weight = jnp.concatenate(
        [jnp.concatenate([e_g.T, low_g.T], axis=1), jnp.concatenate([zero, h_g.T], axis=1)], axis=0
    )
    hi, lo = split(weight)
    wh_ref[...] = hi
    wl_ref[...] = lo
    inv_n = jnp.concatenate(
        [jnp.concatenate([e_n, zero], axis=1), jnp.concatenate([low_n, h_n], axis=1)], axis=0
    )
    upper = jnp.concatenate(
        [jnp.concatenate([u_g, u12_g], axis=1), jnp.concatenate([zero, v_g], axis=1)], axis=0
    )
    project = jnp.concatenate(
        [jnp.concatenate([block(6), block(7)], axis=1), jnp.concatenate([block(8), block(9)], axis=1)], axis=0
    )
    load = jnp.concatenate([x_ref[10 * B : 10 * B + 1, :], x_ref[10 * B + 1 : 10 * B + 2, :]], axis=1)
    load = jnp.broadcast_to(load * (scale * STEP), (8, N))
    turn = dotf(dotf(project, inv_n, (0, 1)), inv_n, (1, 0))
    shift = row_dot(row_dot(load, inv_n, (1, 1)), inv_n, (1, 0))
    index = step_ref[...]
    state = (index == jnp.max(index, axis=1, keepdims=True)).astype(F32)
    now[...] = jnp.broadcast_to(state, (8, N))
    d_ref[...] = jnp.zeros((8, N), F32)
    for i in range(STEPS):
        now[...] = row_dot(now[...], turn, (1, 0)) + shift
        d_ref[i : i + 1, :] = now[:1, :]
    c_ref[...] = row_dot(d_ref[...], upper, (1, 1))[:STEPS, :]


def reduced(total, step_index):
    return pl.pallas_call(
        solve_kernel,
        out_shape=[
            jax.ShapeDtypeStruct((N, N), BF16),
            jax.ShapeDtypeStruct((N, N), BF16),
            jax.ShapeDtypeStruct((8, N), F32),
            jax.ShapeDtypeStruct((STEPS, N), F32),
        ],
        in_specs=[pl.BlockSpec(memory_space=pltpu.VMEM)] * 2,
        out_specs=[pl.BlockSpec(memory_space=pltpu.VMEM)] * 4,
        scratch_shapes=[pltpu.VMEM((8, N), F32)],
        compiler_params=pltpu.CompilerParams(vmem_limit_bytes=24 << 20),
        name="reduced",
    )(total, step_index.reshape(1, N))


def final_kernel(s_ref, y_ref, f_ref, wh_ref, wl_ref, d_ref, basis_ref, res_ref, acc):
    step = pl.program_id(0)
    s = s_ref[...]
    hi, lo = split(s)
    wh = wh_ref[...]
    out = jnp.dot(hi, wh, preferred_element_type=F32)
    out += jnp.dot(lo, wh, preferred_element_type=F32)
    out += jnp.dot(hi, wl_ref[...], preferred_element_type=F32)
    basis_ref[...] = out
    last = d_ref[2:3, :]
    before = d_ref[1:2, :]
    lane = lax.broadcasted_iota(jnp.int32, (B, B), 1)
    for g in range(CHUNK // B):
        rows = slice(g * B, (g + 1) * B)
        z = y_ref[rows, :] * last - s[rows, :] * before
        z = jnp.sum(z[:, :B] + z[:, B:], axis=1, keepdims=True)
        acc[...] = jnp.where(lane == g, z, acc[...])
    res_ref[...] = acc[...].T[: CHUNK // B, :] - STEP * f_ref[...]


def final(snapshots, y, forcing, wh, wl, d):
    rows = snapshots.shape[0]
    whole = lambda i: (0, 0)
    return pl.pallas_call(
        final_kernel,
        grid=(rows // CHUNK,),
        in_specs=[
            pl.BlockSpec((CHUNK, N), lambda i: (i, 0)),
            pl.BlockSpec((CHUNK, N), lambda i: (i, 0)),
            pl.BlockSpec((CHUNK // B, B), lambda i: (i, 0)),
            pl.BlockSpec((N, N), whole),
            pl.BlockSpec((N, N), whole),
            pl.BlockSpec((8, N), whole),
        ],
        out_specs=[
            pl.BlockSpec((CHUNK, N), lambda i: (i, 0)),
            pl.BlockSpec((CHUNK // B, B), lambda i: (i, 0)),
        ],
        out_shape=[
            jax.ShapeDtypeStruct((rows, N), F32),
            jax.ShapeDtypeStruct((rows // B, B), F32),
        ],
        scratch_shapes=[pltpu.VMEM((B, B), F32)],
        compiler_params=pltpu.CompilerParams(vmem_limit_bytes=24 << 20),
        cost_estimate=pl.CostEstimate(flops=6 * rows * N * N, bytes_accessed=12 * rows * N, transcendentals=0),
        name="final",
    )(snapshots, y, forcing, wh, wl, d)


def shifted(value, axis, steps, wrap):
    count = lax.axis_size(axis)
    pairs = [(i, (i + steps) % count) for i in range(count) if wrap or 0 <= i + steps < count]
    return lax.ppermute(value, axis, pairs)


def shards(snapshots, tangent, pattern, forcing, step_index):
    rows = snapshots.shape[0]
    blocks = rows // B
    edge = HALO * B
    tail = snapshots[rows - edge :]
    head = snapshots[:edge]
    halos = (
        shifted(tail, "rows", 1, True),
        shifted(head, "rows", -1, True),
        shifted(tail, "zone", 1, False),
        shifted(head, "zone", -1, False),
    )
    source = pattern // blocks
    block = pattern % blocks
    tail_side = (source == 1) | (source == 3)
    index_map = jnp.where(
        source == 0, block, blocks + HALO * (source - 1) + block - jnp.where(tail_side, blocks - HALO, 0)
    )
    sh, sl, gram_local = gram(snapshots)
    force = forcing.reshape(blocks, B)
    y, pack = image(index_map, tangent, force, gram_local, halos, sh, sl)
    total = reduce_all(pack)
    wh, wl, d, coefficients = reduced(total, step_index)
    basis, residual = final(snapshots, y, force, wh, wl, d)
    return basis, coefficients, residual.reshape(rows)


def solution(mesh):
    both = ("rows", "zone")
    in_specs = (P(both, None), P(both, None), P(both, None), P(both), P())
    out_specs = (P(both, None), P(), P(both))
    return jax.shard_map(shards, mesh=mesh, in_specs=in_specs, out_specs=out_specs, check_vma=False)
```

time: 621 us -> 113 us (0.18)
  waiting for transfers between devices: 212 us -> 7.26 us
  matrix products: 119 us -> 0 us
  other arithmetic: 113 us -> 0.05 us
  Pallas kernels: 0 us -> 78 us
  local copies, waits for them, and re-layouts: 79.5 us -> 13 us
  blocking collectives: 62.9 us -> 0 us
  between operations: 17.5 us -> 0.74 us
    psum x2 -> x0, waiting for transfers between devices: 212 us -> none  [the longest x1 144 us: shards(): gram_matrix = lax.psum(gram_local, ('rows', 'zone'))]
    dot_general x12 -> x0, matrix products: 113 us -> none  [the longest x1 25.2 us: tangent_product(): jnp.einsum('gbec,gecs->gbs', tile_blocks, picked, precision=highest)]
    another operation x22 -> x0, other arithmetic: 109 us -> none  [the longest x7 34.6 us: shards(): normal_low = jnp.linalg.cholesky(normal)]
    pallas_call x0 -> x5, Pallas kernels: none -> 78 us  [the longest x1 25.7 us: reduced(): pl.pallas_call(solve_kernel, out_shape=[jax.ShapeDtypeStruct((N, N), BF16...]
    psum x1 -> x0, blocking collectives: 62.9 us -> none  [shards(): lax.psum((jnp.dot(trial_basis.T, trial_basis, precision=highest) * invers...]
    reshape x2 -> x0, local copies, waits for them, and re-layouts: 24 us -> none  [the longest x1 12.5 us: tangent_product(): tangent.reshape(block_count, block_rows, coupled, block_rows)]
    gather x1 -> x0, local copies, waits for them, and re-layouts: 18.9 us -> none  [tangent_product(): picked = candidates[index_map]]
    mul x1 -> x0, local copies, waits for them, and re-layouts: 8.93 us -> none  [shards(): trial_basis = basis + step_size * tangent_image]
  transfers between devices with their start and end apart: 6 -> 4, of which waited for: 2 -> 1; matrix products, arithmetic and copies ran while one was open for 6% -> 1% of each run, Pallas kernels for 0% -> 3%
where the time goes in v1:
time: 113 us; the launch traced here: 112 us
  Pallas kernels  78 us (69%)
  local copies, waits for them, and re-layouts  13 us (12%)
  starting transfers between devices  13 us (12%)
  waiting for transfers between devices  7.26 us (6%)
    pallas_call x1, Pallas kernels, reduced(): pl.pallas_call(solve_kernel, out_shape=[jax.ShapeDtypeStruct((N, N), BF16...  25.7 us
    pallas_call x1, Pallas kernels, reduce_all(): pl.pallas_call(reduce_kernel, out_shape=jax.ShapeDtypeStruct((PACK, B), F...  24.9 us
    pallas_call x1, Pallas kernels, image(): pl.pallas_call(image_kernel, grid_spec=pltpu.PrefetchScalarGridSpec(num_s...  17.4 us
    ppermute x4, starting transfers between devices, shifted(): return lax.ppermute(value, axis, pairs)  13 us
    unnamed x17, local copies, waits for them, and re-layouts  11.7 us
    ppermute x4, waiting for transfers between devices, shifted(): return lax.ppermute(value, axis, pairs)  7.26 us
    pallas_call x1, Pallas kernels, final(): pl.pallas_call(final_kernel, grid=(rows // CHUNK,), in_specs=[pl.BlockSpe...  6.92 us
    pallas_call x1, Pallas kernels, gram(): pl.pallas_call(gram_kernel, grid=(rows // CHUNK,), in_specs=[pl.BlockSpec...  3.05 us
  transfers between devices with their start and end apart: 4, of which 1 were waited for; matrix products, arithmetic and copies ran while one was open for 1% of the time, Pallas kernels for 3%

profile of v1, /device:TPU:1, one launch (start us, length us, event | category | flops | bytes accessed | tf_op | source)
XLA Modules:
  0.0 112.1 jit_solution(4010359738654424108)
XLA Ops:
  0.6 0.0 copy-start.2
  0.6 1.3 %fusion.1 = (f32[512,256]{1,0:T(8,128)S(1)}, f32[512,256]{1,0:T(8,128)S(1)}) fusion(f32[8192,256]{1,0:T(8,128)} %s_ref.3), kind=kLoop, calls=%fused_computation.8 | loop fusion | bytes 2097152 | tf_op jit(solution)/shard_map/slice | solution.py:447
  1.9 3.3 %collective-permute-start.3 = (f32[512,256]{1,0:T(8,128)S(1)}, f32[512,256]{1,0:T(8,128)S(1)}, u32[]{:S(2)}, u32[]{:S(2)}) collective-permute-start(f32[512,256]{1,0:T(8,128)S(1)} %get-tuple-element.25), channel_id=1, source_target_pairs={{1,0},{2,1},{3,2},{4,3},{5,4},{6,5},{7,6},{9,8},{10,9},{11,10},{12... | collective-permute-start | bytes 1572872 | tf_op jit(solution)/shard_map/ppermute | solution.py:439
  5.3 6.4 %collective-permute-start.1 = (f32[512,256]{1,0:T(8,128)S(1)}, f32[512,256]{1,0:T(8,128)S(1)}, u32[]{:S(2)}, u32[]{:S(2)}) collective-permute-start(f32[512,256]{1,0:T(8,128)S(1)} %get-tuple-element.25), channel_id=1, source_target_pairs={{0,120},{8,0},{16,8},{24,16},{32,24},{40,32},{48,40},{56,48},{64,5... | collective-permute-start | bytes 1572872 | tf_op jit(solution)/shard_map/ppermute | solution.py:439
  11.6 3.3 %collective-permute-start.2 = (f32[512,256]{1,0:T(8,128)S(1)}, f32[512,256]{1,0:T(8,128)S(1)}, u32[]{:S(2)}, u32[]{:S(2)}) collective-permute-start(f32[512,256]{1,0:T(8,128)S(1)} %get-tuple-element.26), channel_id=1, source_target_pairs={{0,1},{1,2},{2,3},{3,4},{4,5},{5,6},{6,7},{8,9},{9,10},{10,11},{11... | collective-permute-start | bytes 1572872 | tf_op jit(solution)/shard_map/ppermute | solution.py:439
  14.9 0.1 collective-permute-start
  15.0 0.8 copy.8
  15.8 0.0 copy-start
  15.8 3.4 %copy-done = f32[8192,256]{1,0:T(8,128)S(1)} copy-done((f32[8192,256]{1,0:T(8,128)S(1)}, f32[8192,256]{1,0:T(8,128)}, u32[]{:S(2)}) %copy-start) | copy-done | bytes 8388632
  19.1 0.0 slice-start
  19.1 3.1 %gram.1 = (bf16[8192,256]{1,0:T(8,128)(2,1)S(1)}, bf16[8192,256]{1,0:T(8,128)(2,1)S(1)}, f32[256,256]{1,0:T(8,128)S(1)}) custom-call(f32[8192,256]{1,0:T(8,128)S(1)} %copy-done), custom_call_target="tpu_custom_call" | custom-call | flops 2147483648 | bytes 16777216 | tf_op jit(solution)/shard_map/gram/pallas_call | solution.py:47
  22.2 0.0 copy-start.4
  22.2 2.0 %copy-done.4 = bf16[8192,256]{1,0:T(8,128)(2,1)} copy-done((bf16[8192,256]{1,0:T(8,128)(2,1)}, bf16[8192,256]{1,0:T(8,128)(2,1)S(1)}, u32[]{:S(2)}) %copy-start.4) | copy-done | bytes 4194328
  24.3 0.0 collective-permute-done.3.zn_ref
  24.3 0.0 collective-permute-done.1.rn_ref
  24.3 0.0 collective-permute-done.2.zp_ref
  24.3 7.3 %collective-permute-done.rp_ref = f32[512,256]{1,0:T(8,128)S(1)} collective-permute-done((f32[512,256]{1,0:T(8,128)S(1)}, f32[512,256]{1,0:T(8,128)S(1)}, u32[]{:S(2)}, u32[]{:S(2)}) %collective-permute-start) | collective-permute-done | bytes 524320 | tf_op jit(solution)/shard_map/ppermute | solution.py:439
  31.6 0.0 copy-done.2
  31.6 0.0 copy-start.5
  31.6 2.2 %copy-done.5 = bf16[8192,256]{1,0:T(8,128)(2,1)S(1)} copy-done((bf16[8192,256]{1,0:T(8,128)(2,1)S(1)}, bf16[8192,256]{1,0:T(8,128)(2,1)}, u32[]{:S(2)}) %copy-start.5) | copy-done | bytes 4194328
  33.7 0.0 copy-start.3
  33.8 0.0 slice-start.1
  33.8 17.4 %image.1 = (f32[8192,256]{1,0:T(8,128)}, f32[1536,128]{1,0:T(8,128)S(1)}) custom-call(s32[64,4]{1,0:T(8,128)S(1)} %subtract_select_fusion.index_ref, bf16[8192,512]{1,0:T(8,128)(2,1)} %t_ref.1, f32[64,128]{1,0:T(8,128)S(1)} %bitcast.5, f32[256,256]{1,0:T(8,128)S(1)} %get-tuple-element.14.g_ref, f32[512,256]{1,0:T(8,128)S(1)} %collective-permute-done.rp_ref, ...), custom_call_target="tpu_custom_call" | custom-call | flops 12884901888 | bytes 33554432 | tf_op jit(solution)/shard_map/image/pallas_call | solution.py:138
  51.1 24.9 %reduce_all.1.x_ref = f32[1536,128]{1,0:T(8,128)S(1)} custom-call(f32[1536,128]{1,0:T(8,128)S(1)} %get-tuple-element.18.x_ref), custom_call_target="tpu_custom_call" | custom-call | tf_op jit(solution)/shard_map/reduce_all/pallas_call | solution.py:261
  76.1 0.0 copy-done.3
  76.1 25.7 %reduced.1 = (bf16[256,256]{1,0:T(8,128)(2,1)S(1)}, bf16[256,256]{1,0:T(8,128)(2,1)S(1)}, f32[8,256]{1,0:T(8,128)S(1)}, f32[3,256]{1,0:T(4,128)}) custom-call(f32[1536,128]{1,0:T(8,128)S(1)} %reduce_all.1.x_ref, s32[1,256]{1,0:T(1,128)S(1)} %bitcast.7), custom_call_target="tpu_custom_call" | custom-call | tf_op jit(solution)/shard_map/reduced/pallas_call | solution.py:371
  101.8 0.0 slice-done
  101.8 0.0 slice-done.1
  101.8 0.0 copy-start.1
  101.8 3.4 %copy-done.1 = f32[8192,256]{1,0:T(8,128)S(1)} copy-done((f32[8192,256]{1,0:T(8,128)S(1)}, f32[8192,256]{1,0:T(8,128)}, u32[]{:S(2)}) %copy-start.1) | copy-done | bytes 8388632
  105.2 6.9 %final.1 = (f32[8192,256]{1,0:T(8,128)}, f32[64,128]{1,0:T(8,128)}) custom-call(f32[8192,256]{1,0:T(8,128)S(1)} %bitcast.4, f32[8192,256]{1,0:T(8,128)S(1)} %copy-done.1, f32[64,128]{1,0:T(8,128)S(1)} %bitcast.6, bf16[256,256]{1,0:T(8,128)(2,1)S(1)} %get-tuple-element.19.wh_ref, bf16[256,256]{1,0:T(8,128)(2,1)S(1)} %get-tuple-element.20.wl_ref, ...), custom_call_target="tpu_custom_call" | custom-call | flops 3221225472 | bytes 25165824 | tf_op jit(solution)/shard_map/final/pallas_call | solution.py:410
  (2 shorter events, 0.0 us)
Async XLA Ops:
  0.6 30.9 %copy-start.2 = (f32[8192]{0:T(1024)S(1)}, f32[8192]{0:T(1024)}, u32[]{:S(2)}) copy-start(f32[8192]{0:T(1024)} %param.8) | copy-start | bytes 98308
  1.9 22.4 %collective-permute-start.3 = (f32[512,256]{1,0:T(8,128)S(1)}, f32[512,256]{1,0:T(8,128)S(1)}, u32[]{:S(2)}, u32[]{:S(2)}) collective-permute-start(f32[512,256]{1,0:T(8,128)S(1)} %get-tuple-element.25), channel_id=1, source_target_pairs={{1,0},{2,1},{3,2},{4,3},{5,4},{6,5},{7,6},{9,8},{10,9},{11,10},{12... | collective-permute-start | bytes 1572872 | tf_op jit(solution)/shard_map/ppermute | solution.py:439
  5.3 19.0 %collective-permute-start.1 = (f32[512,256]{1,0:T(8,128)S(1)}, f32[512,256]{1,0:T(8,128)S(1)}, u32[]{:S(2)}, u32[]{:S(2)}) collective-permute-start(f32[512,256]{1,0:T(8,128)S(1)} %get-tuple-element.25), channel_id=1, source_target_pairs={{0,120},{8,0},{16,8},{24,16},{32,24},{40,32},{48,40},{56,48},{64,5... | collective-permute-start | bytes 1572872 | tf_op jit(solution)/shard_map/ppermute | solution.py:439
  11.6 12.7 %collective-permute-start.2 = (f32[512,256]{1,0:T(8,128)S(1)}, f32[512,256]{1,0:T(8,128)S(1)}, u32[]{:S(2)}, u32[]{:S(2)}) collective-permute-start(f32[512,256]{1,0:T(8,128)S(1)} %get-tuple-element.26), channel_id=1, source_target_pairs={{0,1},{1,2},{2,3},{3,4},{4,5},{5,6},{6,7},{8,9},{9,10},{10,11},{11... | collective-permute-start | bytes 1572872 | tf_op jit(solution)/shard_map/ppermute | solution.py:439
  14.9 16.6 %collective-permute-start = (f32[512,256]{1,0:T(8,128)S(1)}, f32[512,256]{1,0:T(8,128)S(1)}, u32[]{:S(2)}, u32[]{:S(2)}) collective-permute-start(f32[512,256]{1,0:T(8,128)S(1)} %get-tuple-element.26), channel_id=1, source_target_pairs={{0,8},{8,16},{16,24},{24,32},{32,40},{40,48},{48,56},{56,64},{64,7... | collective-permute-start | bytes 1572872 | tf_op jit(solution)/shard_map/ppermute | solution.py:439
  15.8 3.4 %copy-start = (f32[8192,256]{1,0:T(8,128)S(1)}, f32[8192,256]{1,0:T(8,128)}, u32[]{:S(2)}) copy-start(f32[8192,256]{1,0:T(8,128)} %s_ref.3) | copy-start | bytes 25165828
  19.1 82.6 %slice-start = ((s8[8388608]{0:T(1024)(128)(4,1)}), s8[4194304]{0:T(1024)(128)(4,1)S(1)}, s32[]{:S(2)}) async-start(s8[8388608]{0:T(1024)(128)(4,1)} %bitcast.3), calls=%async_computation | async-start | bytes 8388608
  22.2 2.0 %copy-start.4 = (bf16[8192,256]{1,0:T(8,128)(2,1)}, bf16[8192,256]{1,0:T(8,128)(2,1)S(1)}, u32[]{:S(2)}) copy-start(bf16[8192,256]{1,0:T(8,128)(2,1)S(1)} %get-tuple-element.15.sh_hbm) | copy-start | bytes 12582916
  31.6 2.2 %copy-start.5 = (bf16[8192,256]{1,0:T(8,128)(2,1)S(1)}, bf16[8192,256]{1,0:T(8,128)(2,1)}, u32[]{:S(2)}) copy-start(bf16[8192,256]{1,0:T(8,128)(2,1)} %copy-done.4) | copy-start | bytes 12582916
  33.7 42.3 %copy-start.3 = (s32[256]{0:T(256)S(1)}, s32[256]{0:T(256)}, u32[]{:S(2)}) copy-start(s32[256]{0:T(256)} %param.9) | copy-start | bytes 3076
  33.8 68.0 %slice-start.1 = ((s8[8388608]{0:T(1024)(128)(4,1)}), s8[4194304]{0:T(1024)(128)(4,1)S(1)}, s32[]{:S(2)}) async-start(s8[8388608]{0:T(1024)(128)(4,1)} %bitcast.3), calls=%async_computation.1 | async-start | bytes 8388608
  101.8 3.4 %copy-start.1 = (f32[8192,256]{1,0:T(8,128)S(1)}, f32[8192,256]{1,0:T(8,128)}, u32[]{:S(2)}) copy-start(f32[8192,256]{1,0:T(8,128)} %get-tuple-element.17.y_ref) | copy-start | bytes 25165828

commit v2 on v1

--- a/solution.py
+++ b/solution.py
@@ -29,63 +29,94 @@
     return lax.dot_general(a, b, (((0,), (0,)), ((), ())), preferred_element_type=F32)
 
 
-def gram_kernel(s_ref, sh_ref, sl_ref, g_ref):
+def front_kernel(s_hbm, ch_ref, cl_ref, g_ref, sbuf, halo, load_sem, send_sem, recv_sem):
+    rows = s_hbm.shape[0]
+    edge = HALO * B
+    chunks = rows // CHUNK
+    ring, belt = lax.axis_size("rows"), lax.axis_size("zone")
+    row_id, zone_id = lax.axis_index("rows"), lax.axis_index("zone")
+    loads = []
+    for i in range(chunks):
+        part = pl.ds(i * CHUNK, CHUNK)
+        loads.append(pltpu.make_async_copy(s_hbm.at[part], sbuf.at[part], load_sem.at[i]))
+        loads[-1].start()
+    peers = (
+        ((row_id + 1) % ring, zone_id),
+        ((row_id + ring - 1) % ring, zone_id),
+        (row_id, (zone_id + 1) % belt),
+        (row_id, (zone_id + belt - 1) % belt),
+    )
+    barrier = pltpu.get_barrier_semaphore()
+    for peer in peers:
+        pl.semaphore_signal(barrier, inc=1, device_id=peer, device_id_type=MESH)
+    pl.semaphore_wait(barrier, 4)
+    copies = []
+    for i, peer in enumerate(peers):
+        start = rows - edge if i % 2 == 0 else 0
+        copies.append(
+            pltpu.make_async_remote_copy(
+                src_ref=s_hbm.at[pl.ds(start, edge)], dst_ref=halo.at[i],
+                send_sem=send_sem.at[i], recv_sem=recv_sem.at[i], device_id=peer, device_id_type=MESH,
+            )
+        )
+        copies[-1].start()
+    total = jnp.zeros((N, N), F32)
+    for i in range(chunks):
+        loads[i].wait()
+        part = pl.ds(i * CHUNK, CHUNK)
+        hi, lo = split(sbuf[part, :])
+        ch_ref[part, :] = hi
+        cl_ref[part, :] = lo
+        total += tdot(hi, hi)
+    g_ref[...] = total
+    there = (True, True, zone_id > 0, zone_id < belt - 1)
+    for i in (2, 3, 0, 1):
+        copies[i].wait_recv()
+        value = halo[i]
+        if i >= 2:
+            value = jnp.where(there[i], value, 0.0)
+        hi, lo = split(value)
+        part = pl.ds(rows + i * edge, edge)
+        ch_ref[part, :] = hi
+        cl_ref[part, :] = lo
+    for copy in copies:
+        copy.wait_send()
+
+
+def front(snapshots):
+    rows = snapshots.shape[0]
+    edge = HALO * B
+    return pl.pallas_call(
+        front_kernel,
+        in_specs=[pl.BlockSpec(memory_space=pl.ANY)],
+        out_specs=[pl.BlockSpec(memory_space=pltpu.VMEM)] * 3,
+        out_shape=[
+            jax.ShapeDtypeStruct((rows + 4 * edge, N), BF16),
+            jax.ShapeDtypeStruct((rows + 4 * edge, N), BF16),
+            jax.ShapeDtypeStruct((N, N), F32),
+        ],
+        scratch_shapes=[
+            pltpu.VMEM((rows, N), F32),
+            pltpu.VMEM((4, edge, N), F32),
+            pltpu.SemaphoreType.DMA((rows // CHUNK,)),
+            pltpu.SemaphoreType.DMA((4,)),
+            pltpu.SemaphoreType.DMA((4,)),
+        ],
+        compiler_params=pltpu.CompilerParams(collective_id=1, has_side_effects=True, vmem_limit_bytes=38 << 20),
+        cost_estimate=pl.CostEstimate(flops=2 * rows * N * N, bytes_accessed=8 * rows * N, transcendentals=0),
+        name="front",
+    )(snapshots)
+
+
+def image_kernel(
+    index_ref, t_ref, f_ref, g_ref, cand_h, cand_l, y_ref, pack_ref, left, right, acc, load_acc,
+):
     step = pl.program_id(0)
 
     @pl.when(step == 0)
     def _():
-        g_ref[...] = jnp.zeros_like(g_ref)
-
-    hi, lo = split(s_ref[...])
-    sh_ref[...] = hi
-    sl_ref[...] = lo
-    g_ref[...] += tdot(hi, hi)
-
-
-def gram(snapshots):
-    rows = snapshots.shape[0]
-    return pl.pallas_call(
-        gram_kernel,
-        grid=(rows // CHUNK,),
-        in_specs=[pl.BlockSpec((CHUNK, N), lambda i: (i, 0))],
-        out_specs=[
-            pl.BlockSpec((CHUNK, N), lambda i: (i, 0)),
-            pl.BlockSpec((CHUNK, N), lambda i: (i, 0)),
-            pl.BlockSpec((N, N), lambda i: (0, 0)),
-        ],
-        out_shape=[
-            jax.ShapeDtypeStruct((rows, N), BF16),
-            jax.ShapeDtypeStruct((rows, N), BF16),
-            jax.ShapeDtypeStruct((N, N), F32),
-        ],
-        compiler_params=pltpu.CompilerParams(vmem_limit_bytes=24 << 20),
-        cost_estimate=pl.CostEstimate(flops=4 * rows * N * N, bytes_accessed=8 * rows * N, transcendentals=0),
-        name="gram",
-    )(snapshots)
-
-
-def image_kernel(
-    index_ref, t_ref, f_ref, g_ref, rp_ref, rn_ref, zp_ref, zn_ref, sh_hbm, sl_hbm, y_ref, pack_ref,
-    cand_h, cand_l, left, right, acc, load_acc, sem,
-):
-    step = pl.program_id(0)
-    rows = sh_hbm.shape[0]
-    edge = HALO * B
-
-    @pl.when(step == 0)
-    def _():
-        one = pltpu.make_async_copy(sh_hbm, cand_h.at[pl.ds(0, rows)], sem.at[0])
-        two = pltpu.make_async_copy(sl_hbm, cand_l.at[pl.ds(0, rows)], sem.at[1])
-        one.start()
-        two.start()
-        for i, ref in enumerate((rp_ref, rn_ref, zp_ref, zn_ref)):
-            hi, lo = split(ref[...])
-            cand_h[pl.ds(rows + i * edge, edge), :] = hi
-            cand_l[pl.ds(rows + i * edge, edge), :] = lo
         acc[...] = jnp.zeros_like(acc)
         load_acc[...] = jnp.zeros_like(load_acc)
-        one.wait()
-        two.wait()
 
     groups = CHUNK // B
     force = f_ref[...].T
@@ -97,7 +128,7 @@
         image += jnp.dot(tiles, jnp.concatenate([cand_l[p, :] for p in picks], axis=0), preferred_element_type=F32)
         own = pl.ds(pl.multiple_of(step * CHUNK + g * B, B), B)
         y = cand_h[own, :].astype(F32) + cand_l[own, :].astype(F32) + STEP * image
-        y_ref[g * B : (g + 1) * B, :] = y
+        y_ref[own, :] = y
         hi, lo = split(y)
         left[g * B : (g + 1) * B, :N] = hi
         left[g * B : (g + 1) * B, N : 2 * N] = lo
@@ -131,9 +162,8 @@
         pack_ref[10 * B + 1 : 10 * B + 2, :] = load[:, B:]
 
 
-def image(index_map, tangent, forcing, gram_local, halos, sh, sl):
-    rows = sh.shape[0]
-    edge = HALO * B
+def image(index_map, tangent, forcing, gram_local, cand_h, cand_l):
+    rows = tangent.shape[0]
     whole = lambda i, *_: (0, 0)
     return pl.pallas_call(
         image_kernel,
@@ -143,32 +173,29 @@
             in_specs=[
                 pl.BlockSpec((CHUNK, 4 * B), lambda i, *_: (i, 0)),
                 pl.BlockSpec((CHUNK // B, B), lambda i, *_: (i, 0)),
-                pl.BlockSpec((N, N), whole, pipeline_mode=pl.Buffered(1)),
-            ]
-            + [pl.BlockSpec((edge, N), whole, pipeline_mode=pl.Buffered(1))] * 4
-            + [pl.BlockSpec(memory_space=pl.ANY)] * 2,
+                pl.BlockSpec(memory_space=pltpu.VMEM),
+                pl.BlockSpec(memory_space=pltpu.VMEM),
+                pl.BlockSpec(memory_space=pltpu.VMEM),
+            ],
             out_specs=[
-                pl.BlockSpec((CHUNK, N), lambda i, *_: (i, 0)),
+                pl.BlockSpec(memory_space=pltpu.VMEM),
                 pl.BlockSpec((PACK, B), whole),
             ],
             scratch_shapes=[
-                pltpu.VMEM((rows + 4 * edge, N), BF16),
-                pltpu.VMEM((rows + 4 * edge, N), BF16),
                 pltpu.VMEM((CHUNK, 3 * N), BF16),
                 pltpu.VMEM((CHUNK, 2 * N), BF16),
                 pltpu.VMEM((4, N, N), F32),
                 pltpu.VMEM((8, N), F32),
-                pltpu.SemaphoreType.DMA((2,)),
             ],
         ),
         out_shape=[
             jax.ShapeDtypeStruct((rows, N), F32),
             jax.ShapeDtypeStruct((PACK, B), F32),
         ],
-        compiler_params=pltpu.CompilerParams(vmem_limit_bytes=40 << 20),
-        cost_estimate=pl.CostEstimate(flops=24 * rows * N * N, bytes_accessed=16 * rows * N, transcendentals=0),
+        compiler_params=pltpu.CompilerParams(vmem_limit_bytes=28 << 20),
+        cost_estimate=pl.CostEstimate(flops=20 * rows * N * N, bytes_accessed=8 * rows * N, transcendentals=0),
         name="image",
-    )(index_map, tangent, forcing, gram_local, *halos, sh, sl)
+    )(index_map, tangent, forcing, gram_local, cand_h, cand_l)
 
 
 PARTS = 3
@@ -384,10 +411,11 @@
     )(total, step_index.reshape(1, N))
 
 
-def final_kernel(s_ref, y_ref, f_ref, wh_ref, wl_ref, d_ref, basis_ref, res_ref, acc):
+def final_kernel(ch_ref, cl_ref, y_ref, f_ref, wh_ref, wl_ref, d_ref, basis_ref, res_ref, acc):
     step = pl.program_id(0)
-    s = s_ref[...]
-    hi, lo = split(s)
+    here = pl.ds(pl.multiple_of(step * CHUNK, CHUNK), CHUNK)
+    hi = ch_ref[here, :]
+    lo = cl_ref[here, :]
     wh = wh_ref[...]
     out = jnp.dot(hi, wh, preferred_element_type=F32)
     out += jnp.dot(lo, wh, preferred_element_type=F32)
@@ -397,22 +425,22 @@
     before = d_ref[1:2, :]
     lane = lax.broadcasted_iota(jnp.int32, (B, B), 1)
     for g in range(CHUNK // B):
-        rows = slice(g * B, (g + 1) * B)
-        z = y_ref[rows, :] * last - s[rows, :] * before
+        own = pl.ds(pl.multiple_of(step * CHUNK + g * B, B), B)
+        s = ch_ref[own, :].astype(F32) + cl_ref[own, :].astype(F32)
+        z = y_ref[own, :] * last - s * before
         z = jnp.sum(z[:, :B] + z[:, B:], axis=1, keepdims=True)
         acc[...] = jnp.where(lane == g, z, acc[...])
     res_ref[...] = acc[...].T[: CHUNK // B, :] - STEP * f_ref[...]
 
 
-def final(snapshots, y, forcing, wh, wl, d):
-    rows = snapshots.shape[0]
+def final(cand_h, cand_l, y, forcing, wh, wl, d):
+    rows = y.shape[0]
     whole = lambda i: (0, 0)
     return pl.pallas_call(
         final_kernel,
         grid=(rows // CHUNK,),
-        in_specs=[
-            pl.BlockSpec((CHUNK, N), lambda i: (i, 0)),
-            pl.BlockSpec((CHUNK, N), lambda i: (i, 0)),
+        in_specs=[pl.BlockSpec(memory_space=pltpu.VMEM)] * 3
+        + [
             pl.BlockSpec((CHUNK // B, B), lambda i: (i, 0)),
             pl.BlockSpec((N, N), whole),
             pl.BlockSpec((N, N), whole),
@@ -427,42 +455,27 @@
             jax.ShapeDtypeStruct((rows // B, B), F32),
         ],
         scratch_shapes=[pltpu.VMEM((B, B), F32)],
-        compiler_params=pltpu.CompilerParams(vmem_limit_bytes=24 << 20),
+        compiler_params=pltpu.CompilerParams(vmem_limit_bytes=28 << 20),
         cost_estimate=pl.CostEstimate(flops=6 * rows * N * N, bytes_accessed=12 * rows * N, transcendentals=0),
         name="final",
-    )(snapshots, y, forcing, wh, wl, d)
-
-
-def shifted(value, axis, steps, wrap):
-    count = lax.axis_size(axis)
-    pairs = [(i, (i + steps) % count) for i in range(count) if wrap or 0 <= i + steps < count]
-    return lax.ppermute(value, axis, pairs)
+    )(cand_h, cand_l, y, forcing, wh, wl, d)
 
 
 def shards(snapshots, tangent, pattern, forcing, step_index):
     rows = snapshots.shape[0]
     blocks = rows // B
-    edge = HALO * B
-    tail = snapshots[rows - edge :]
-    head = snapshots[:edge]
-    halos = (
-        shifted(tail, "rows", 1, True),
-        shifted(head, "rows", -1, True),
-        shifted(tail, "zone", 1, False),
-        shifted(head, "zone", -1, False),
-    )
     source = pattern // blocks
     block = pattern % blocks
     tail_side = (source == 1) | (source == 3)
     index_map = jnp.where(
         source == 0, block, blocks + HALO * (source - 1) + block - jnp.where(tail_side, blocks - HALO, 0)
     )
-    sh, sl, gram_local = gram(snapshots)
+    cand_h, cand_l, gram_local = front(snapshots)
     force = forcing.reshape(blocks, B)
-    y, pack = image(index_map, tangent, force, gram_local, halos, sh, sl)
+    y, pack = image(index_map, tangent, force, gram_local, cand_h, cand_l)
     total = reduce_all(pack)
     wh, wl, d, coefficients = reduced(total, step_index)
-    basis, residual = final(snapshots, y, force, wh, wl, d)
+    basis, residual = final(cand_h, cand_l, y, force, wh, wl, d)
     return basis, coefficients, residual.reshape(rows)
 
 

time: 113 us -> 96.2 us (0.85)
  Pallas kernels: 78 us -> 94.5 us
  starting transfers between devices: 13 us -> 0 us
  local copies, waits for them, and re-layouts: 13 us -> 0.79 us
  waiting for transfers between devices: 7.26 us -> 0 us
    pallas_call x1, Pallas kernels: 3.05 us -> 20.6 us  [front(): pl.pallas_call(front_kernel, in_specs=[pl.BlockSpec(memory_space=pl.ANY)]...]
    ppermute x4 -> x0, starting transfers between devices: 13 us -> none  [shifted(): return lax.ppermute(value, axis, pairs)]
    unnamed x17 -> x5, local copies, waits for them, and re-layouts: 11.7 us -> 0.79 us
    ppermute x4 -> x0, waiting for transfers between devices: 7.26 us -> none  [shifted(): return lax.ppermute(value, axis, pairs)]
    pallas_call x1, Pallas kernels: 17.4 us -> 15.7 us  [image(): pl.pallas_call(image_kernel, grid_spec=pltpu.PrefetchScalarGridSpec(num_s...]
    slice x1 -> x0, local copies, waits for them, and re-layouts: 1.27 us -> none  [shards(): head = snapshots[:edge]]
  transfers between devices with their start and end apart: 4 -> 0, of which waited for: 1 -> 0; matrix products, arithmetic and copies ran while one was open for 1% -> 0% of each run, Pallas kernels for 3% -> 0%
where the time goes in v2:
time: 96.2 us; the launch traced here: 96 us
  Pallas kernels  94.5 us (98%)
    pallas_call x1, Pallas kernels, reduce_all(): pl.pallas_call(reduce_kernel, out_shape=jax.ShapeDtypeStruct((PACK, B), F...  25.7 us
    pallas_call x1, Pallas kernels, reduced(): pl.pallas_call(solve_kernel, out_shape=[jax.ShapeDtypeStruct((N, N), BF16...  25.7 us
    pallas_call x1, Pallas kernels, front(): pl.pallas_call(front_kernel, in_specs=[pl.BlockSpec(memory_space=pl.ANY)]...  20.6 us
    pallas_call x1, Pallas kernels, image(): pl.pallas_call(image_kernel, grid_spec=pltpu.PrefetchScalarGridSpec(num_s...  15.7 us
    pallas_call x1, Pallas kernels, final(): pl.pallas_call(final_kernel, grid=(rows // CHUNK,), in_specs=[pl.BlockSpe...  6.8 us

profile of v2, /device:TPU:1, one launch (start us, length us, event | category | flops | bytes accessed | tf_op | source)
XLA Modules:
  0.0 96.0 jit_solution(16837087458612075178)
XLA Ops:
  0.6 0.0 copy-start
  0.6 0.8 copy.8
  1.5 20.6 %front.1 = (bf16[10240,256]{1,0:T(8,128)(2,1)S(1)}, bf16[10240,256]{1,0:T(8,128)(2,1)S(1)}, f32[256,256]{1,0:T(8,128)S(1)}) custom-call(f32[8192,256]{1,0:T(8,128)} %s_hbm.1), custom_call_target="tpu_custom_call" | custom-call | flops 1073741824 | bytes 16777216 | tf_op jit(solution)/shard_map/front/pallas_call | solution.py:89
  22.0 0.0 copy-done
  22.0 0.0 copy-start.1
  22.0 15.7 %image.1 = (f32[8192,256]{1,0:T(8,128)S(1)}, f32[1536,128]{1,0:T(8,128)S(1)}) custom-call(s32[64,4]{1,0:T(8,128)S(1)} %subtract_select_fusion.index_ref, bf16[8192,512]{1,0:T(8,128)(2,1)} %t_ref.1, f32[64,128]{1,0:T(8,128)S(1)} %bitcast.3, f32[256,256]{1,0:T(8,128)S(1)} %get-tuple-element.16.g_ref, bf16[10240,256]{1,0:T(8,128)(2,1)S(1)} %get-tuple-element.14.cand_h.ch_ref, ...), custom_call_target="tpu_custom_call" | custom-call | flops 10737418240 | bytes 16777216 | tf_op jit(solution)/shard_map/image/pallas_call | solution.py:168
  37.7 25.7 %reduce_all.1.x_ref = f32[1536,128]{1,0:T(8,128)S(1)} custom-call(f32[1536,128]{1,0:T(8,128)S(1)} %get-tuple-element.18.x_ref), custom_call_target="tpu_custom_call" | custom-call | tf_op jit(solution)/shard_map/reduce_all/pallas_call | solution.py:288
  63.5 0.0 copy-done.1
  63.5 25.7 %reduced.1 = (bf16[256,256]{1,0:T(8,128)(2,1)S(1)}, bf16[256,256]{1,0:T(8,128)(2,1)S(1)}, f32[8,256]{1,0:T(8,128)S(1)}, f32[3,256]{1,0:T(4,128)}) custom-call(f32[1536,128]{1,0:T(8,128)S(1)} %reduce_all.1.x_ref, s32[1,256]{1,0:T(1,128)S(1)} %bitcast.5), custom_call_target="tpu_custom_call" | custom-call | tf_op jit(solution)/shard_map/reduced/pallas_call | solution.py:398
  89.2 6.8 %final.1 = (f32[8192,256]{1,0:T(8,128)}, f32[64,128]{1,0:T(8,128)}) custom-call(bf16[10240,256]{1,0:T(8,128)(2,1)S(1)} %get-tuple-element.14.cand_h.ch_ref, bf16[10240,256]{1,0:T(8,128)(2,1)S(1)} %get-tuple-element.15.cand_l.cl_ref, f32[8192,256]{1,0:T(8,128)S(1)} %get-tuple-element.17.y_ref, f32[64,128]{1,0:T(8,128)S(1)} %bitcast.4, ...), custom_call_target="tpu_custom_call" | custom-call | flops 3221225472 | bytes 25165824 | tf_op jit(solution)/shard_map/final/pallas_call | solution.py:439
  (1 shorter events, 0.0 us)
Async XLA Ops:
  0.6 21.4 %copy-start = (f32[8192]{0:T(1024)S(1)}, f32[8192]{0:T(1024)}, u32[]{:S(2)}) copy-start(f32[8192]{0:T(1024)} %param.8) | copy-start | bytes 98308
  22.0 41.5 %copy-start.1 = (s32[256]{0:T(256)S(1)}, s32[256]{0:T(256)}, u32[]{:S(2)}) copy-start(s32[256]{0:T(256)} %param.9) | copy-start | bytes 3076

commit v3 on v2

--- a/solution.py
+++ b/solution.py
@@ -13,7 +13,7 @@
 B = 128
 N = 256
 CHUNK = 1024
-PACK = 1536
+PACK = 1344
 F32 = jnp.float32
 BF16 = jnp.bfloat16
 HI = lax.Precision.HIGHEST
@@ -60,15 +60,16 @@
             )
         )
         copies[-1].start()
-    total = jnp.zeros((N, N), F32)
+    total = jnp.zeros((2 * N, N), F32)
     for i in range(chunks):
         loads[i].wait()
         part = pl.ds(i * CHUNK, CHUNK)
         hi, lo = split(sbuf[part, :])
         ch_ref[part, :] = hi
         cl_ref[part, :] = lo
-        total += tdot(hi, hi)
-    g_ref[...] = total
+        total += tdot(jnp.concatenate([hi, lo], axis=1), hi)
+    half = total[:N] * 0.5 + total[N:]
+    g_ref[...] = half + half.T
     there = (True, True, zone_id > 0, zone_id < belt - 1)
     for i in (2, 3, 0, 1):
         copies[i].wait_recv()
@@ -109,7 +110,7 @@
 
 
 def image_kernel(
-    index_ref, t_ref, f_ref, g_ref, cand_h, cand_l, y_ref, pack_ref, left, right, acc, load_acc,
+    index_ref, t_ref, f_ref, g_ref, cand_h, cand_l, y_ref, pack_ref, ybuf_h, ybuf_l, acc, load_acc,
 ):
     step = pl.program_id(0)
 
@@ -130,26 +131,24 @@
         y = cand_h[own, :].astype(F32) + cand_l[own, :].astype(F32) + STEP * image
         y_ref[own, :] = y
         hi, lo = split(y)
-        left[g * B : (g + 1) * B, :N] = hi
-        left[g * B : (g + 1) * B, N : 2 * N] = lo
-        right[g * B : (g + 1) * B, N:] = hi
+        ybuf_h[g * B : (g + 1) * B, :] = hi
+        ybuf_l[g * B : (g + 1) * B, :] = lo
         total += jnp.sum((y * force[:, g : g + 1]).reshape(B // 8, 8, N), axis=0)
     load_acc[...] += total
     here = pl.ds(pl.multiple_of(step * CHUNK, CHUNK), CHUNK)
-    left[:, 2 * N :] = cand_l[here, :]
-    right[:, :N] = cand_h[here, :]
-    both = tdot(left[...], right[...])
-    acc[0] += both[:N, :N] + both[N : 2 * N, :N]
-    acc[1] += both[:N, N:] * 0.5 + both[N : 2 * N, N:]
-    acc[2] += both[2 * N :, N:]
-    acc[3] += both[2 * N :, :N]
+    yh = ybuf_h[...]
+    yl = ybuf_l[...]
+    one = tdot(jnp.concatenate([yh, yl], axis=1), cand_h[here, :])
+    acc[0] += one[:N] + one[N:]
+    two = tdot(jnp.concatenate([yh, yl, cand_l[here, :]], axis=1), yh)
+    acc[1] += two[:N] * 0.5 + two[N : 2 * N]
+    acc[2] += two[2 * N :]
 
     @pl.when(step == pl.num_programs(0) - 1)
     def _():
         normal = acc[1] + acc[1].T
         project = acc[0] + acc[2].T
-        half = g_ref[...] * 0.5 + acc[3]
-        gram_matrix = half + half.T
+        gram_matrix = g_ref[...]
         blocks = []
         for matrix in (gram_matrix, normal):
             blocks += [matrix[:B, :B], matrix[:B, B:], matrix[B:, B:]]
@@ -182,9 +181,9 @@
                 pl.BlockSpec((PACK, B), whole),
             ],
             scratch_shapes=[
-                pltpu.VMEM((CHUNK, 3 * N), BF16),
-                pltpu.VMEM((CHUNK, 2 * N), BF16),
-                pltpu.VMEM((4, N, N), F32),
+                pltpu.VMEM((CHUNK, N), BF16),
+                pltpu.VMEM((CHUNK, N), BF16),
+                pltpu.VMEM((3, N, N), F32),
                 pltpu.VMEM((8, N), F32),
             ],
         ),
@@ -200,11 +199,11 @@
 
 PARTS = 3
 PART = PACK // PARTS
-STAGE_SLOTS = (1, 3, 3, 3, 3, 3, 1)
-STAGE_BASE = tuple(PARTS * sum(STAGE_SLOTS[:i]) for i in range(7))
-
-
-def reduce_kernel(x_ref, o_ref, acc1, acc2, got0, got1, got2, got3, send_sem, recv_sem):
+STAGE_SLOTS = (1, 3, 3, 3, 3, 1)
+STAGE_BASE = tuple(PARTS * sum(STAGE_SLOTS[:i]) for i in range(6))
+
+
+def reduce_kernel(x_ref, o_ref, acc, got0, got1, got2, got3, send_sem, recv_sem):
     rows_id = lax.axis_index("rows")
     zone_id = lax.axis_index("zone")
     core = zone_id % 2
@@ -240,44 +239,39 @@
 
     half = PART // 2
     quarter = half // 4
-    piece = quarter // 4
     mine = core * half
     for p in range(PARTS):
         send(0, p, 0, x_ref.at[pl.ds(p * PART + (1 - core) * half, half)], got0.at[p], "core", 1)
     for p, (a, b, c) in enumerate(orders):
         arrive(0, p)
-        acc1[p] = x_ref[pl.ds(p * PART + mine, half), :] + got0[p]
+        acc[p] = x_ref[pl.ds(p * PART + mine, half), :] + got0[p]
         for o in (1, 2, 3):
             there = (place[a] + o) % 4
-            send(1, p, o - 1, acc1.at[p, pl.ds(there * quarter, quarter)], got1.at[p, o - 1], a, o)
+            send(1, p, o - 1, acc.at[p, pl.ds(there * quarter, quarter)], got1.at[p, o - 1], a, o)
     for p, (a, b, c) in enumerate(orders):
         arrive(1, p)
-        acc2[p] = acc1[p, pl.ds(place[a] * quarter, quarter), :] + got1[p, 0] + got1[p, 1] + got1[p, 2]
+        slot = got2.at[p, place[b]]
+        slot[...] = acc[p, pl.ds(place[a] * quarter, quarter), :] + got1[p, 0] + got1[p, 1] + got1[p, 2]
         for o in (1, 2, 3):
-            there = (place[b] + o) % 4
-            send(2, p, o - 1, acc2.at[p, pl.ds(there * piece, piece)], got2.at[p, o - 1], b, o)
+            send(2, p, o - 1, slot, slot, b, o)
     for p, (a, b, c) in enumerate(orders):
         arrive(2, p)
-        got3[p, place[c]] = acc2[p, pl.ds(place[b] * piece, piece), :] + got2[p, 0] + got2[p, 1] + got2[p, 2]
+        slot = got3.at[p, place[c]]
+        slot[...] = got2[p, 0] + got2[p, 1] + got2[p, 2] + got2[p, 3]
         for o in (1, 2, 3):
-            send(3, p, o - 1, got3.at[p, place[c]], got3.at[p, place[c]], c, o)
+            send(3, p, o - 1, slot, slot, c, o)
     for p, (a, b, c) in enumerate(orders):
         arrive(3, p)
-        spot = p * PART + mine + place[a] * quarter + place[b] * piece
-        o_ref[pl.ds(spot, piece), :] = got3[p, 0] + got3[p, 1] + got3[p, 2] + got3[p, 3]
+        spot = o_ref.at[pl.ds(p * PART + mine + place[a] * quarter, quarter)]
+        spot[...] = got3[p, 0] + got3[p, 1] + got3[p, 2] + got3[p, 3]
         for o in (1, 2, 3):
-            send(4, p, o - 1, o_ref.at[pl.ds(spot, piece)], o_ref.at[pl.ds(spot, piece)], b, o)
-    for p, (a, b, c) in enumerate(orders):
+            send(4, p, o - 1, spot, spot, a, o)
+    for p in range(PARTS):
         arrive(4, p)
-        spot = p * PART + mine + place[a] * quarter
-        for o in (1, 2, 3):
-            send(5, p, o - 1, o_ref.at[pl.ds(spot, quarter)], o_ref.at[pl.ds(spot, quarter)], a, o)
+        spot = o_ref.at[pl.ds(p * PART + mine, half)]
+        send(5, p, 0, spot, spot, "core", 1)
     for p in range(PARTS):
         arrive(5, p)
-        spot = p * PART + mine
-        send(6, p, 0, o_ref.at[pl.ds(spot, half)], o_ref.at[pl.ds(spot, half)], "core", 1)
-    for p in range(PARTS):
-        arrive(6, p)
     for copy in live.values():
         copy.wait_send()
 
@@ -292,17 +286,22 @@
         out_specs=pl.BlockSpec(memory_space=pltpu.VMEM),
         scratch_shapes=[
             pltpu.VMEM((PARTS, half, B), F32),
-            pltpu.VMEM((PARTS, half // 4, B), F32),
             pltpu.VMEM((PARTS, half, B), F32),
             pltpu.VMEM((PARTS, 3, half // 4, B), F32),
-            pltpu.VMEM((PARTS, 3, half // 16, B), F32),
-            pltpu.VMEM((PARTS, 4, half // 16, B), F32),
+            pltpu.VMEM((PARTS, 4, half // 4, B), F32),
+            pltpu.VMEM((PARTS, 4, half // 4, B), F32),
             pltpu.SemaphoreType.DMA((count,)),
             pltpu.SemaphoreType.DMA((count,)),
         ],
         compiler_params=pltpu.CompilerParams(collective_id=0, has_side_effects=True, vmem_limit_bytes=16 << 20),
         name="reduce_all",
     )(pack)
+
+
+def split3f(x):
+    hi = x.astype(BF16).astype(F32)
+    mid = (x - hi).astype(BF16).astype(F32)
+    return hi, mid, (x - hi - mid)
 
 
 def factor_blocks(matrices):
@@ -310,21 +309,46 @@
     lane = lax.broadcasted_iota(jnp.int32, (8, B), 1)
     sub = lax.broadcasted_iota(jnp.int32, (8, B), 0)
     inverse = [[(lane == sub + 8 * t).astype(F32) for t in range(16)] for _ in matrices]
-    for k in range(B):
-        t0, i = divmod(k, 8)
+    for p in range(16):
         for a, e in zip(tiles, inverse):
-            pivot = lax.rsqrt(a[t0][i : i + 1, k : k + 1])
-            row = a[t0][i : i + 1, :] * pivot
-            erow = e[t0][i : i + 1, :] * pivot
-            for t in range(t0, 16):
-                scale = a[t][:, k : k + 1] * pivot
-                new_a = a[t] - scale * row
-                new_e = e[t] - scale * erow
-                if t == t0:
-                    new_a = jnp.where(sub > i, new_a, jnp.where(sub == i, row, a[t]))
-                    new_e = jnp.where(sub > i, new_e, jnp.where(sub == i, erow, e[t]))
-                a[t] = new_a
-                e[t] = new_e
+            spread = lambda t: [jnp.broadcast_to(a[t][:, 8 * p + c : 8 * p + c + 1], (8, B)) for c in range(8)]
+            column = spread(p)
+            pivot, link = [], {}
+            for k in range(8):
+                pivot.append(lax.rsqrt(column[k][k : k + 1, :]))
+                column[k] = column[k] * pivot[k]
+                for c in range(k + 1, 8):
+                    link[k, c] = column[k][c : c + 1, :]
+                    column[c] = column[c] - column[k] * link[k, c]
+            rows, erows = [], []
+            own, eown = a[p], e[p]
+            for k in range(8):
+                rows.append(own[k : k + 1, :] * pivot[k])
+                erows.append(eown[k : k + 1, :] * pivot[k])
+                own = own - column[k] * rows[k]
+                eown = eown - column[k] * erows[k]
+            if p + 1 < 16:
+                t = p + 1
+                column = spread(t)
+                for k in range(8):
+                    column[k] = column[k] * pivot[k]
+                    for c in range(k + 1, 8):
+                        column[c] = column[c] - column[k] * link[k, c]
+                    a[t] = a[t] - column[k] * rows[k]
+                    e[t] = e[t] - column[k] * erows[k]
+            a[p] = jnp.concatenate(rows, axis=0)
+            e[p] = jnp.concatenate(erows, axis=0)
+            if p + 2 < 16:
+                ah, am, al = split3f(a[p])
+                eh, em, el = split3f(e[p])
+                lhs = jnp.concatenate([ah, ah, am, ah, al, am], axis=0).astype(BF16)
+                rhs = jnp.concatenate(
+                    [jnp.concatenate([ah, am, ah, al, ah, am], axis=0), jnp.concatenate([eh, em, eh, el, eh, em], axis=0)], axis=1
+                ).astype(BF16)
+                update = tdot(lhs, rhs)
+                for t in range(p + 2, 16):
+                    a[t] = a[t] - update[8 * t : 8 * t + 8, :B]
+                    e[t] = e[t] - update[8 * t : 8 * t + 8, B:]
     upper = [
         jnp.concatenate([jnp.where(lane >= sub + 8 * t, a[t], 0.0) for t in range(16)], axis=0) for a in tiles
     ]
@@ -381,9 +405,10 @@
         [jnp.concatenate([block(6), block(7)], axis=1), jnp.concatenate([block(8), block(9)], axis=1)], axis=0
     )
     load = jnp.concatenate([x_ref[10 * B : 10 * B + 1, :], x_ref[10 * B + 1 : 10 * B + 2, :]], axis=1)
-    load = jnp.broadcast_to(load * (scale * STEP), (8, N))
-    turn = dotf(dotf(project, inv_n, (0, 1)), inv_n, (1, 0))
-    shift = row_dot(row_dot(load, inv_n, (1, 1)), inv_n, (1, 0))
+    stack = jnp.concatenate([project.T, jnp.broadcast_to(load * (scale * STEP), (8, N))], axis=0)
+    stack = dotf(dotf(stack, inv_n, (1, 1)), inv_n, (1, 0))
+    turn = stack[:N]
+    shift = stack[N:]
     index = step_ref[...]
     state = (index == jnp.max(index, axis=1, keepdims=True)).astype(F32)
     now[...] = jnp.broadcast_to(state, (8, N))

time: 96.2 us -> 78.1 us (0.81)
  Pallas kernels: 94.5 us -> 76.3 us
    pallas_call x1, Pallas kernels: 25.7 us -> 11.1 us  [reduced(): pl.pallas_call(solve_kernel, out_shape=[jax.ShapeDtypeStruct((N, N), BF16...]
    pallas_call x1, Pallas kernels: 25.7 us -> 23.4 us  [reduce_all(): pl.pallas_call(reduce_kernel, out_shape=jax.ShapeDtypeStruct((PACK, B), F...]
    pallas_call x1, Pallas kernels: 15.7 us -> 14.5 us  [image(): pl.pallas_call(image_kernel, grid_spec=pltpu.PrefetchScalarGridSpec(num_s...]
where the time goes in v3:
time: 78.1 us; the launch traced here: 77.9 us
  Pallas kernels  76.3 us (98%)
  local copies, waits for them, and re-layouts  0.79 us (1%)
    pallas_call x1, Pallas kernels, reduce_all(): pl.pallas_call(reduce_kernel, out_shape=jax.ShapeDtypeStruct((PACK, B), F...  23.4 us
    pallas_call x1, Pallas kernels, front(): pl.pallas_call(front_kernel, in_specs=[pl.BlockSpec(memory_space=pl.ANY)]...  20.6 us
    pallas_call x1, Pallas kernels, image(): pl.pallas_call(image_kernel, grid_spec=pltpu.PrefetchScalarGridSpec(num_s...  14.5 us
    pallas_call x1, Pallas kernels, reduced(): pl.pallas_call(solve_kernel, out_shape=[jax.ShapeDtypeStruct((N, N), BF16...  11.1 us
    pallas_call x1, Pallas kernels, final(): pl.pallas_call(final_kernel, grid=(rows // CHUNK,), in_specs=[pl.BlockSpe...  6.8 us

profile of v3, /device:TPU:1, one launch (start us, length us, event | category | flops | bytes accessed | tf_op | source)
XLA Modules:
  0.0 77.9 jit_solution(14967336861249007087)
XLA Ops:
  0.6 0.0 copy-start
  0.6 0.8 copy.8
  1.5 20.6 %front.1 = (bf16[10240,256]{1,0:T(8,128)(2,1)S(1)}, bf16[10240,256]{1,0:T(8,128)(2,1)S(1)}, f32[256,256]{1,0:T(8,128)S(1)}) custom-call(f32[8192,256]{1,0:T(8,128)} %s_hbm.1), custom_call_target="tpu_custom_call" | custom-call | flops 1073741824 | bytes 16777216 | tf_op jit(solution)/shard_map/front/pallas_call | solution.py:90
  22.0 0.0 copy-done
  22.0 0.0 copy-start.1
  22.0 14.5 %image.1 = (f32[8192,256]{1,0:T(8,128)S(1)}, f32[1344,128]{1,0:T(8,128)S(1)}) custom-call(s32[64,4]{1,0:T(8,128)S(1)} %subtract_select_fusion.index_ref, bf16[8192,512]{1,0:T(8,128)(2,1)} %t_ref.1, f32[64,128]{1,0:T(8,128)S(1)} %bitcast.3, f32[256,256]{1,0:T(8,128)S(1)} %get-tuple-element.16.g_ref, bf16[10240,256]{1,0:T(8,128)(2,1)S(1)} %get-tuple-element.14.cand_h.ch_ref, ...), custom_call_target="tpu_custom_call" | custom-call | flops 10737418240 | bytes 16777216 | tf_op jit(solution)/shard_map/image/pallas_call | solution.py:167
  36.5 23.4 %reduce_all.1.x_ref = f32[1344,128]{1,0:T(8,128)S(1)} custom-call(f32[1344,128]{1,0:T(8,128)S(1)} %get-tuple-element.18.x_ref), custom_call_target="tpu_custom_call" | custom-call | tf_op jit(solution)/shard_map/reduce_all/pallas_call | solution.py:282
  59.9 0.0 copy-done.1
  60.0 11.1 %reduced.1 = (bf16[256,256]{1,0:T(8,128)(2,1)S(1)}, bf16[256,256]{1,0:T(8,128)(2,1)S(1)}, f32[8,256]{1,0:T(8,128)S(1)}, f32[3,256]{1,0:T(4,128)}) custom-call(f32[1344,128]{1,0:T(8,128)S(1)} %reduce_all.1.x_ref, s32[1,256]{1,0:T(1,128)S(1)} %bitcast.5), custom_call_target="tpu_custom_call" | custom-call | tf_op jit(solution)/shard_map/reduced/pallas_call | solution.py:423
  71.1 6.8 %final.1 = (f32[8192,256]{1,0:T(8,128)}, f32[64,128]{1,0:T(8,128)}) custom-call(bf16[10240,256]{1,0:T(8,128)(2,1)S(1)} %get-tuple-element.14.cand_h.ch_ref, bf16[10240,256]{1,0:T(8,128)(2,1)S(1)} %get-tuple-element.15.cand_l.cl_ref, f32[8192,256]{1,0:T(8,128)S(1)} %get-tuple-element.17.y_ref, f32[64,128]{1,0:T(8,128)S(1)} %bitcast.4, ...), custom_call_target="tpu_custom_call" | custom-call | flops 3221225472 | bytes 25165824 | tf_op jit(solution)/shard_map/final/pallas_call | solution.py:464
  (1 shorter events, 0.0 us)
Async XLA Ops:
  0.6 21.4 %copy-start = (f32[8192]{0:T(1024)S(1)}, f32[8192]{0:T(1024)}, u32[]{:S(2)}) copy-start(f32[8192]{0:T(1024)} %param.8) | copy-start | bytes 98308
  22.0 37.9 %copy-start.1 = (s32[256]{0:T(256)S(1)}, s32[256]{0:T(256)}, u32[]{:S(2)}) copy-start(s32[256]{0:T(256)} %param.9) | copy-start | bytes 3076

commit v4 on v3

--- a/solution.py
+++ b/solution.py
@@ -65,8 +65,9 @@
         loads[i].wait()
         part = pl.ds(i * CHUNK, CHUNK)
         hi, lo = split(sbuf[part, :])
-        ch_ref[part, :] = hi
-        cl_ref[part, :] = lo
+        spot = pl.ds(i * CHUNK // B, CHUNK // B)
+        ch_ref[spot] = hi.reshape(CHUNK // B, B, N)
+        cl_ref[spot] = lo.reshape(CHUNK // B, B, N)
         total += tdot(jnp.concatenate([hi, lo], axis=1), hi)
     half = total[:N] * 0.5 + total[N:]
     g_ref[...] = half + half.T
@@ -77,9 +78,9 @@
         if i >= 2:
             value = jnp.where(there[i], value, 0.0)
         hi, lo = split(value)
-        part = pl.ds(rows + i * edge, edge)
-        ch_ref[part, :] = hi
-        cl_ref[part, :] = lo
+        spot = pl.ds(rows // B + i * HALO, HALO)
+        ch_ref[spot] = hi.reshape(HALO, B, N)
+        cl_ref[spot] = lo.reshape(HALO, B, N)
     for copy in copies:
         copy.wait_send()
 
@@ -92,8 +93,8 @@
         in_specs=[pl.BlockSpec(memory_space=pl.ANY)],
         out_specs=[pl.BlockSpec(memory_space=pltpu.VMEM)] * 3,
         out_shape=[
-            jax.ShapeDtypeStruct((rows + 4 * edge, N), BF16),
-            jax.ShapeDtypeStruct((rows + 4 * edge, N), BF16),
+            jax.ShapeDtypeStruct((rows // B + 4 * HALO, B, N), BF16),
+            jax.ShapeDtypeStruct((rows // B + 4 * HALO, B, N), BF16),
             jax.ShapeDtypeStruct((N, N), F32),
         ],
         scratch_shapes=[
@@ -109,107 +110,17 @@
     )(snapshots)
 
 
-def image_kernel(
-    index_ref, t_ref, f_ref, g_ref, cand_h, cand_l, y_ref, pack_ref, ybuf_h, ybuf_l, acc, load_acc,
-):
-    step = pl.program_id(0)
-
-    @pl.when(step == 0)
-    def _():
-        acc[...] = jnp.zeros_like(acc)
-        load_acc[...] = jnp.zeros_like(load_acc)
-
-    groups = CHUNK // B
-    force = f_ref[...].T
-    total = jnp.zeros((8, N), F32)
-    for g in range(groups):
-        picks = [pl.ds(pl.multiple_of(index_ref[step * groups + g, e] * B, B), B) for e in range(4)]
-        tiles = t_ref[g * B : (g + 1) * B, :]
-        image = jnp.dot(tiles, jnp.concatenate([cand_h[p, :] for p in picks], axis=0), preferred_element_type=F32)
-        image += jnp.dot(tiles, jnp.concatenate([cand_l[p, :] for p in picks], axis=0), preferred_element_type=F32)
-        own = pl.ds(pl.multiple_of(step * CHUNK + g * B, B), B)
-        y = cand_h[own, :].astype(F32) + cand_l[own, :].astype(F32) + STEP * image
-        y_ref[own, :] = y
-        hi, lo = split(y)
-        ybuf_h[g * B : (g + 1) * B, :] = hi
-        ybuf_l[g * B : (g + 1) * B, :] = lo
-        total += jnp.sum((y * force[:, g : g + 1]).reshape(B // 8, 8, N), axis=0)
-    load_acc[...] += total
-    here = pl.ds(pl.multiple_of(step * CHUNK, CHUNK), CHUNK)
-    yh = ybuf_h[...]
-    yl = ybuf_l[...]
-    one = tdot(jnp.concatenate([yh, yl], axis=1), cand_h[here, :])
-    acc[0] += one[:N] + one[N:]
-    two = tdot(jnp.concatenate([yh, yl, cand_l[here, :]], axis=1), yh)
-    acc[1] += two[:N] * 0.5 + two[N : 2 * N]
-    acc[2] += two[2 * N :]
-
-    @pl.when(step == pl.num_programs(0) - 1)
-    def _():
-        normal = acc[1] + acc[1].T
-        project = acc[0] + acc[2].T
-        gram_matrix = g_ref[...]
-        blocks = []
-        for matrix in (gram_matrix, normal):
-            blocks += [matrix[:B, :B], matrix[:B, B:], matrix[B:, B:]]
-        blocks += [project[:B, :B], project[:B, B:], project[B:, :B], project[B:, B:]]
-        for i, block in enumerate(blocks):
-            pack_ref[i * B : (i + 1) * B, :] = block
-        load = jnp.sum(load_acc[...], axis=0, keepdims=True)
-        pack_ref[10 * B :, :] = jnp.zeros((PACK - 10 * B, B), F32)
-        pack_ref[10 * B : 10 * B + 1, :] = load[:, :B]
-        pack_ref[10 * B + 1 : 10 * B + 2, :] = load[:, B:]
-
-
-def image(index_map, tangent, forcing, gram_local, cand_h, cand_l):
-    rows = tangent.shape[0]
-    whole = lambda i, *_: (0, 0)
-    return pl.pallas_call(
-        image_kernel,
-        grid_spec=pltpu.PrefetchScalarGridSpec(
-            num_scalar_prefetch=1,
-            grid=(rows // CHUNK,),
-            in_specs=[
-                pl.BlockSpec((CHUNK, 4 * B), lambda i, *_: (i, 0)),
-                pl.BlockSpec((CHUNK // B, B), lambda i, *_: (i, 0)),
-                pl.BlockSpec(memory_space=pltpu.VMEM),
-                pl.BlockSpec(memory_space=pltpu.VMEM),
-                pl.BlockSpec(memory_space=pltpu.VMEM),
-            ],
-            out_specs=[
-                pl.BlockSpec(memory_space=pltpu.VMEM),
-                pl.BlockSpec((PACK, B), whole),
-            ],
-            scratch_shapes=[
-                pltpu.VMEM((CHUNK, N), BF16),
-                pltpu.VMEM((CHUNK, N), BF16),
-                pltpu.VMEM((3, N, N), F32),
-                pltpu.VMEM((8, N), F32),
-            ],
-        ),
-        out_shape=[
-            jax.ShapeDtypeStruct((rows, N), F32),
-            jax.ShapeDtypeStruct((PACK, B), F32),
-        ],
-        compiler_params=pltpu.CompilerParams(vmem_limit_bytes=28 << 20),
-        cost_estimate=pl.CostEstimate(flops=20 * rows * N * N, bytes_accessed=8 * rows * N, transcendentals=0),
-        name="image",
-    )(index_map, tangent, forcing, gram_local, cand_h, cand_l)
-
-
 PARTS = 3
 PART = PACK // PARTS
 STAGE_SLOTS = (1, 3, 3, 3, 3, 1)
 STAGE_BASE = tuple(PARTS * sum(STAGE_SLOTS[:i]) for i in range(6))
 
 
-def reduce_kernel(x_ref, o_ref, acc, got0, got1, got2, got3, send_sem, recv_sem):
+def reach():
     rows_id = lax.axis_index("rows")
     zone_id = lax.axis_index("zone")
     core = zone_id % 2
     place = {"x": zone_id // 2, "y": rows_id % 4, "z": rows_id // 4}
-    orders = (("x", "y", "z"), ("y", "z", "x"), ("z", "x", "y"))
-
     def device(axis, shift):
         at = dict(place)
         if axis == "core":
@@ -217,11 +128,19 @@
         at[axis] = (at[axis] + shift) % 4
         return (at["z"] * 4 + at["y"], at["x"] * 2 + core)
 
+    return core, place, device
+
+
+def greet():
+    _, _, device = reach()
     barrier = pltpu.get_barrier_semaphore()
     for axis, shift in [("core", 1)] + [(a, s) for a in "xyz" for s in (1, 2, 3)]:
         pl.semaphore_signal(barrier, inc=1, device_id=device(axis, shift), device_id_type=MESH)
-    pl.semaphore_wait(barrier, 10)
-
+
+
+def reduce_all(x_ref, o_ref, acc, got0, got1, got2, got3, send_sem, recv_sem):
+    core, place, device = reach()
+    pl.semaphore_wait(pltpu.get_barrier_semaphore(), 10)
     live = {}
 
     def send(stage, part, slot, src, dst, axis, shift):
@@ -237,6 +156,7 @@
         for slot in range(STAGE_SLOTS[stage]):
             live[stage, part, slot].wait_recv()
 
+    orders = (("x", "y", "z"), ("y", "z", "x"), ("z", "x", "y"))
     half = PART // 2
     quarter = half // 4
     mine = core * half
@@ -276,26 +196,106 @@
         copy.wait_send()
 
 
-def reduce_all(pack):
+def image_kernel(
+    index_ref, t_ref, f_ref, g_ref, cand_h, cand_l, y_ref, total_ref,
+    ybuf_h, ybuf_l, acc, load_acc, pack_ref, *exchange,
+):
+    step = pl.program_id(0)
+
+    @pl.when(step == 0)
+    def _():
+        greet()
+        acc[...] = jnp.zeros_like(acc)
+        load_acc[...] = jnp.zeros_like(load_acc)
+
+    groups = CHUNK // B
+    force = f_ref[...].T
+    total = jnp.zeros((8, N), F32)
+    for g in range(groups):
+        picks = [index_ref[e, step * groups + g] for e in range(4)]
+        tiles = t_ref[g * B : (g + 1) * B, :]
+        image = jnp.dot(tiles, jnp.concatenate([cand_h[p] for p in picks], axis=0), preferred_element_type=F32)
+        image += jnp.dot(tiles, jnp.concatenate([cand_l[p] for p in picks], axis=0), preferred_element_type=F32)
+        own = pl.ds(pl.multiple_of(step * CHUNK + g * B, B), B)
+        y = cand_h[step * groups + g].astype(F32) + cand_l[step * groups + g].astype(F32) + STEP * image
+        y_ref[own, :] = y
+        hi, lo = split(y)
+        ybuf_h[g * B : (g + 1) * B, :] = hi
+        ybuf_l[g * B : (g + 1) * B, :] = lo
+        total += jnp.sum((y * force[:, g : g + 1]).reshape(B // 8, 8, N), axis=0)
+    load_acc[...] += total
+    here = pl.ds(step * groups, groups)
+    yh = ybuf_h[...]
+    yl = ybuf_l[...]
+    one = tdot(jnp.concatenate([yh, yl], axis=1), cand_h[here].reshape(CHUNK, N))
+    acc[0] += one[:N] + one[N:]
+    two = tdot(jnp.concatenate([yh, yl, cand_l[here].reshape(CHUNK, N)], axis=1), yh)
+    acc[1] += two[:N] * 0.5 + two[N : 2 * N]
+    acc[2] += two[2 * N :]
+
+    @pl.when(step == pl.num_programs(0) - 1)
+    def _():
+        normal = acc[1] + acc[1].T
+        project = acc[0] + acc[2].T
+        gram_matrix = g_ref[...]
+        blocks = []
+        for matrix in (gram_matrix, normal):
+            blocks += [matrix[:B, :B], matrix[:B, B:], matrix[B:, B:]]
+        blocks += [project[:B, :B], project[:B, B:], project[B:, :B], project[B:, B:]]
+        for i, block in enumerate(blocks):
+            pack_ref[i * B : (i + 1) * B, :] = block
+        load = jnp.sum(load_acc[...], axis=0, keepdims=True)
+        pack_ref[10 * B :, :] = jnp.zeros((PACK - 10 * B, B), F32)
+        pack_ref[10 * B : 10 * B + 1, :] = load[:, :B]
+        pack_ref[10 * B + 1 : 10 * B + 2, :] = load[:, B:]
+        reduce_all(pack_ref, *exchange)
+        total_ref[...] = exchange[0][...]
+
+
+def image(index_map, tangent, forcing, gram_local, cand_h, cand_l):
+    rows = tangent.shape[0]
     half = PART // 2
     count = PARTS * sum(STAGE_SLOTS)
     return pl.pallas_call(
-        reduce_kernel,
-        out_shape=jax.ShapeDtypeStruct((PACK, B), F32),
-        in_specs=[pl.BlockSpec(memory_space=pltpu.VMEM)],
-        out_specs=pl.BlockSpec(memory_space=pltpu.VMEM),
-        scratch_shapes=[
-            pltpu.VMEM((PARTS, half, B), F32),
-            pltpu.VMEM((PARTS, half, B), F32),
-            pltpu.VMEM((PARTS, 3, half // 4, B), F32),
-            pltpu.VMEM((PARTS, 4, half // 4, B), F32),
-            pltpu.VMEM((PARTS, 4, half // 4, B), F32),
-            pltpu.SemaphoreType.DMA((count,)),
-            pltpu.SemaphoreType.DMA((count,)),
-        ],
-        compiler_params=pltpu.CompilerParams(collective_id=0, has_side_effects=True, vmem_limit_bytes=16 << 20),
-        name="reduce_all",
-    )(pack)
+        image_kernel,
+        grid_spec=pltpu.PrefetchScalarGridSpec(
+            num_scalar_prefetch=1,
+            grid=(rows // CHUNK,),
+            in_specs=[
+                pl.BlockSpec((CHUNK, 4 * B), lambda i, *_: (i, 0)),
+                pl.BlockSpec((CHUNK // B, B), lambda i, *_: (i, 0)),
+                pl.BlockSpec(memory_space=pltpu.VMEM),
+                pl.BlockSpec(memory_space=pltpu.VMEM),
+                pl.BlockSpec(memory_space=pltpu.VMEM),
+            ],
+            out_specs=[
+                pl.BlockSpec(memory_space=pltpu.VMEM),
+                pl.BlockSpec(memory_space=pltpu.VMEM),
+            ],
+            scratch_shapes=[
+                pltpu.VMEM((CHUNK, N), BF16),
+                pltpu.VMEM((CHUNK, N), BF16),
+                pltpu.VMEM((3, N, N), F32),
+                pltpu.VMEM((8, N), F32),
+                pltpu.VMEM((PACK, B), F32),
+                pltpu.VMEM((PACK, B), F32),
+                pltpu.VMEM((PARTS, half, B), F32),
+                pltpu.VMEM((PARTS, half, B), F32),
+                pltpu.VMEM((PARTS, 3, half // 4, B), F32),
+                pltpu.VMEM((PARTS, 4, half // 4, B), F32),
+                pltpu.VMEM((PARTS, 4, half // 4, B), F32),
+                pltpu.SemaphoreType.DMA((count,)),
+                pltpu.SemaphoreType.DMA((count,)),
+            ],
+        ),
+        out_shape=[
+            jax.ShapeDtypeStruct((rows, N), F32),
+            jax.ShapeDtypeStruct((PACK, B), F32),
+        ],
+        compiler_params=pltpu.CompilerParams(collective_id=0, has_side_effects=True, vmem_limit_bytes=28 << 20),
+        cost_estimate=pl.CostEstimate(flops=20 * rows * N * N, bytes_accessed=8 * rows * N, transcendentals=0),
+        name="image",
+    )(index_map, tangent, forcing, gram_local, cand_h, cand_l)
 
 
 def split3f(x):
@@ -367,13 +367,13 @@
 
 
 def row_dot(a, b, dims):
-    left, right = split3(a), split3(b)
-    total = jnp.zeros((8, N), F32)
-    for i, j in ((2, 0), (1, 1), (0, 2), (1, 0), (0, 1), (0, 0)):
-        total += lax.dot_general(
-            left[i], right[j], ((dims[:1], dims[1:]), ((), ())), preferred_element_type=F32
-        )
-    return total
+    hi, mid, low = split3(a)
+    dot = lambda x, y: lax.dot_general(x, y, ((dims[:1], dims[1:]), ((), ())), preferred_element_type=F32)
+    rows = [t.astype(F32) for t in (hi, mid, low)]
+    one = dot(jnp.concatenate(rows, axis=0).astype(BF16), b[0])
+    two = dot(jnp.concatenate(rows[:2], axis=0).astype(BF16), b[1])
+    three = dot(hi, b[2])
+    return (one[16:] + two[8:16] + three) + (one[8:16] + two[:8]) + one[:8]
 
 
 def solve_kernel(x_ref, step_ref, wh_ref, wl_ref, d_ref, c_ref, now):
@@ -410,13 +410,17 @@
     turn = stack[:N]
     shift = stack[N:]
     index = step_ref[...]
-    state = (index == jnp.max(index, axis=1, keepdims=True)).astype(F32)
-    now[...] = jnp.broadcast_to(state, (8, N))
+    lane = lax.broadcasted_iota(jnp.int32, (1, N), 1)
+    latest = jnp.sum(jnp.where(index == jnp.max(index, axis=1, keepdims=True), lane, 0), axis=1, keepdims=True)
+    chosen = lax.broadcasted_iota(jnp.int32, (N, N), 0) == latest
+    now[...] = jnp.sum(jnp.where(chosen, turn, 0.0), axis=0, keepdims=True) + shift
     d_ref[...] = jnp.zeros((8, N), F32)
-    for i in range(STEPS):
-        now[...] = row_dot(now[...], turn, (1, 0)) + shift
+    d_ref[0:1, :] = now[:1, :]
+    terms = split3(turn)
+    for i in range(1, STEPS):
+        now[...] = row_dot(now[...], terms, (1, 0)) + shift
         d_ref[i : i + 1, :] = now[:1, :]
-    c_ref[...] = row_dot(d_ref[...], upper, (1, 1))[:STEPS, :]
+    c_ref[...] = row_dot(d_ref[...], split3(upper), (1, 1))[:STEPS, :]
 
 
 def reduced(total, step_index):
@@ -438,9 +442,10 @@
 
 def final_kernel(ch_ref, cl_ref, y_ref, f_ref, wh_ref, wl_ref, d_ref, basis_ref, res_ref, acc):
     step = pl.program_id(0)
-    here = pl.ds(pl.multiple_of(step * CHUNK, CHUNK), CHUNK)
-    hi = ch_ref[here, :]
-    lo = cl_ref[here, :]
+    groups = CHUNK // B
+    here = pl.ds(step * groups, groups)
+    hi = ch_ref[here].reshape(CHUNK, N)
+    lo = cl_ref[here].reshape(CHUNK, N)
     wh = wh_ref[...]
     out = jnp.dot(hi, wh, preferred_element_type=F32)
     out += jnp.dot(lo, wh, preferred_element_type=F32)
@@ -451,7 +456,7 @@
     lane = lax.broadcasted_iota(jnp.int32, (B, B), 1)
     for g in range(CHUNK // B):
         own = pl.ds(pl.multiple_of(step * CHUNK + g * B, B), B)
-        s = ch_ref[own, :].astype(F32) + cl_ref[own, :].astype(F32)
+        s = ch_ref[step * groups + g].astype(F32) + cl_ref[step * groups + g].astype(F32)
         z = y_ref[own, :] * last - s * before
         z = jnp.sum(z[:, :B] + z[:, B:], axis=1, keepdims=True)
         acc[...] = jnp.where(lane == g, z, acc[...])
@@ -489,16 +494,16 @@
 def shards(snapshots, tangent, pattern, forcing, step_index):
     rows = snapshots.shape[0]
     blocks = rows // B
-    source = pattern // blocks
-    block = pattern % blocks
+    codes = pattern.T
+    source = codes // blocks
+    block = codes % blocks
     tail_side = (source == 1) | (source == 3)
     index_map = jnp.where(
         source == 0, block, blocks + HALO * (source - 1) + block - jnp.where(tail_side, blocks - HALO, 0)
     )
     cand_h, cand_l, gram_local = front(snapshots)
     force = forcing.reshape(blocks, B)
-    y, pack = image(index_map, tangent, force, gram_local, cand_h, cand_l)
-    total = reduce_all(pack)
+    y, total = image(index_map, tangent, force, gram_local, cand_h, cand_l)
     wh, wl, d, coefficients = reduced(total, step_index)
     basis, residual = final(cand_h, cand_l, y, force, wh, wl, d)
     return basis, coefficients, residual.reshape(rows)

time: 78.1 us -> 75 us (0.960)
  Pallas kernels: 76.3 us -> 73.4 us
    pallas_call x1 -> x0, Pallas kernels: 23.4 us -> none  [reduce_all(): pl.pallas_call(reduce_kernel, out_shape=jax.ShapeDtypeStruct((PACK, B), F...]
    pallas_call x1, Pallas kernels: 14.5 us -> 35.4 us  [image(): pl.pallas_call(image_kernel, grid_spec=pltpu.PrefetchScalarGridSpec(num_s...]
where the time goes in v4:
time: 75 us; the launch traced here: 74.8 us
  Pallas kernels  73.4 us (98%)
    pallas_call x1, Pallas kernels, image(): pl.pallas_call(image_kernel, grid_spec=pltpu.PrefetchScalarGridSpec(num_s...  35.4 us
    pallas_call x1, Pallas kernels, front(): pl.pallas_call(front_kernel, in_specs=[pl.BlockSpec(memory_space=pl.ANY)]...  20.6 us
    pallas_call x1, Pallas kernels, reduced(): pl.pallas_call(solve_kernel, out_shape=[jax.ShapeDtypeStruct((N, N), BF16...  10.6 us
    pallas_call x1, Pallas kernels, final(): pl.pallas_call(final_kernel, grid=(rows // CHUNK,), in_specs=[pl.BlockSpe...  6.88 us

profile of v4, /device:TPU:1, one launch (start us, length us, event | category | flops | bytes accessed | tf_op | source)
XLA Modules:
  0.0 74.8 jit_solution(1284375798754945994)
XLA Ops:
  0.6 0.0 copy-start
  0.6 0.7 subtract_select_fusion.index_ref
  1.3 20.6 %front.1 = (bf16[80,128,256]{2,1,0:T(8,128)(2,1)S(1)}, bf16[80,128,256]{2,1,0:T(8,128)(2,1)S(1)}, f32[256,256]{1,0:T(8,128)S(1)}) custom-call(f32[8192,256]{1,0:T(8,128)} %s_hbm.1), custom_call_target="tpu_custom_call" | custom-call | flops 1073741824 | bytes 16777216 | tf_op jit(solution)/shard_map/front/pallas_call | solution.py:91
  21.9 0.0 copy-done
  21.9 0.0 copy-start.1
  21.9 35.4 %image.1 = (f32[8192,256]{1,0:T(8,128)S(1)}, f32[1344,128]{1,0:T(8,128)S(1)}) custom-call(s32[4,64]{1,0:T(4,128)S(1)} %subtract_select_fusion.index_ref, bf16[8192,512]{1,0:T(8,128)(2,1)} %t_ref.1, f32[64,128]{1,0:T(8,128)S(1)} %bitcast.21, f32[256,256]{1,0:T(8,128)S(1)} %get-tuple-element.16.g_ref, ...), custom_call_target="tpu_custom_call" | custom-call | flops 10737418240 | bytes 16777216 | tf_op jit(solution)/shard_map/image/pallas_call | solution.py:259
  57.3 0.0 copy-done.1
  57.3 10.6 %reduced.1 = (bf16[256,256]{1,0:T(8,128)(2,1)S(1)}, bf16[256,256]{1,0:T(8,128)(2,1)S(1)}, f32[8,256]{1,0:T(8,128)S(1)}, f32[3,256]{1,0:T(4,128)}) custom-call(f32[1344,128]{1,0:T(8,128)S(1)} %get-tuple-element.18.x_ref, s32[1,256]{1,0:T(1,128)S(1)} %bitcast.23), custom_call_target="tpu_custom_call" | custom-call | tf_op jit(solution)/shard_map/reduced/pallas_call | solution.py:427
  68.0 6.9 %final.1 = (f32[8192,256]{1,0:T(8,128)}, f32[64,128]{1,0:T(8,128)}) custom-call(bf16[80,128,256]{2,1,0:T(8,128)(2,1)S(1)} %get-tuple-element.14.cand_h.ch_ref, bf16[80,128,256]{2,1,0:T(8,128)(2,1)S(1)} %get-tuple-element.15.cand_l.cl_ref, f32[8192,256]{1,0:T(8,128)S(1)} %get-tuple-element.17.y_ref, f32[64,128]{1,0:T(8,128)S(1)} %bitcast.22, ...), custom_call_target="tpu_custom_call" | custom-call | flops 3221225472 | bytes 25165824 | tf_op jit(solution)/shard_map/final/pallas_call | solution.py:469
Async XLA Ops:
  0.6 21.3 %copy-start = (f32[8192]{0:T(1024)S(1)}, f32[8192]{0:T(1024)}, u32[]{:S(2)}) copy-start(f32[8192]{0:T(1024)} %param.8) | copy-start | bytes 98308
  21.9 35.4 %copy-start.1 = (s32[256]{0:T(256)S(1)}, s32[256]{0:T(256)}, u32[]{:S(2)}) copy-start(s32[256]{0:T(256)} %param.9) | copy-start | bytes 3076

commit v5 on v4

--- a/solution.py
+++ b/solution.py
@@ -196,8 +196,15 @@
         copy.wait_send()
 
 
+def decode(code, blocks):
+    source = code // blocks
+    block = code % blocks
+    tail = jnp.where((source == 1) | (source == 3), blocks - HALO, 0)
+    return jnp.where(source == 0, block, blocks + HALO * (source - 1) + block - tail)
+
+
 def image_kernel(
-    index_ref, t_ref, f_ref, g_ref, cand_h, cand_l, y_ref, total_ref,
+    code_ref, t_ref, f_ref, g_ref, cand_h, cand_l, y_ref, total_ref,
     ybuf_h, ybuf_l, acc, load_acc, pack_ref, *exchange,
 ):
     step = pl.program_id(0)
@@ -212,7 +219,7 @@
     force = f_ref[...].T
     total = jnp.zeros((8, N), F32)
     for g in range(groups):
-        picks = [index_ref[e, step * groups + g] for e in range(4)]
+        picks = [decode(code_ref[e, step * groups + g], cand_h.shape[0] - 4 * HALO) for e in range(4)]
         tiles = t_ref[g * B : (g + 1) * B, :]
         image = jnp.dot(tiles, jnp.concatenate([cand_h[p] for p in picks], axis=0), preferred_element_type=F32)
         image += jnp.dot(tiles, jnp.concatenate([cand_l[p] for p in picks], axis=0), preferred_element_type=F32)
@@ -252,7 +259,7 @@
         total_ref[...] = exchange[0][...]
 
 
-def image(index_map, tangent, forcing, gram_local, cand_h, cand_l):
+def image(codes, tangent, forcing, gram_local, cand_h, cand_l):
     rows = tangent.shape[0]
     half = PART // 2
     count = PARTS * sum(STAGE_SLOTS)
@@ -295,7 +302,7 @@
         compiler_params=pltpu.CompilerParams(collective_id=0, has_side_effects=True, vmem_limit_bytes=28 << 20),
         cost_estimate=pl.CostEstimate(flops=20 * rows * N * N, bytes_accessed=8 * rows * N, transcendentals=0),
         name="image",
-    )(index_map, tangent, forcing, gram_local, cand_h, cand_l)
+    )(codes, tangent, forcing, gram_local, cand_h, cand_l)
 
 
 def split3f(x):
@@ -376,7 +383,7 @@
     return (one[16:] + two[8:16] + three) + (one[8:16] + two[:8]) + one[:8]
 
 
-def solve_kernel(x_ref, step_ref, wh_ref, wl_ref, d_ref, c_ref, now):
+def factor_step(x_ref, weight, inverse, stack, upper):
     scale = 1.0 / (8192 * 128)
     block = lambda i: x_ref[i * B : (i + 1) * B, :] * scale
     g11, g12, g22, n11, n12, n22 = (block(i) for i in range(6))
@@ -389,123 +396,130 @@
     low_g = -dotf(h_g, dotf(u12_g, e_g, (0, 0)), (1, 0))
     low_n = -dotf(h_n, dotf(u12_n, e_n, (0, 0)), (1, 0))
     zero = jnp.zeros((B, B), F32)
-    weight = jnp.concatenate(
-        [jnp.concatenate([e_g.T, low_g.T], axis=1), jnp.concatenate([zero, h_g.T], axis=1)], axis=0
+    hi, lo = split(
+        jnp.concatenate(
+            [jnp.concatenate([e_g.T, low_g.T], axis=1), jnp.concatenate([zero, h_g.T], axis=1)], axis=0
+        )
     )
-    hi, lo = split(weight)
-    wh_ref[...] = hi
-    wl_ref[...] = lo
-    inv_n = jnp.concatenate(
+    weight[:N, :] = hi
+    weight[N : 2 * N, :] = hi
+    weight[2 * N :, :] = lo
+    inverse[...] = jnp.concatenate(
         [jnp.concatenate([e_n, zero], axis=1), jnp.concatenate([low_n, h_n], axis=1)], axis=0
     )
-    upper = jnp.concatenate(
+    upper[...] = jnp.concatenate(
         [jnp.concatenate([u_g, u12_g], axis=1), jnp.concatenate([zero, v_g], axis=1)], axis=0
     )
     project = jnp.concatenate(
         [jnp.concatenate([block(6), block(7)], axis=1), jnp.concatenate([block(8), block(9)], axis=1)], axis=0
     )
     load = jnp.concatenate([x_ref[10 * B : 10 * B + 1, :], x_ref[10 * B + 1 : 10 * B + 2, :]], axis=1)
-    stack = jnp.concatenate([project.T, jnp.broadcast_to(load * (scale * STEP), (8, N))], axis=0)
-    stack = dotf(dotf(stack, inv_n, (1, 1)), inv_n, (1, 0))
-    turn = stack[:N]
-    shift = stack[N:]
-    index = step_ref[...]
-    lane = lax.broadcasted_iota(jnp.int32, (1, N), 1)
-    latest = jnp.sum(jnp.where(index == jnp.max(index, axis=1, keepdims=True), lane, 0), axis=1, keepdims=True)
-    chosen = lax.broadcasted_iota(jnp.int32, (N, N), 0) == latest
-    now[...] = jnp.sum(jnp.where(chosen, turn, 0.0), axis=0, keepdims=True) + shift
-    d_ref[...] = jnp.zeros((8, N), F32)
-    d_ref[0:1, :] = now[:1, :]
-    terms = split3(turn)
-    for i in range(1, STEPS):
-        now[...] = row_dot(now[...], terms, (1, 0)) + shift
-        d_ref[i : i + 1, :] = now[:1, :]
-    c_ref[...] = row_dot(d_ref[...], split3(upper), (1, 1))[:STEPS, :]
-
-
-def reduced(total, step_index):
-    return pl.pallas_call(
-        solve_kernel,
-        out_shape=[
-            jax.ShapeDtypeStruct((N, N), BF16),
-            jax.ShapeDtypeStruct((N, N), BF16),
-            jax.ShapeDtypeStruct((8, N), F32),
-            jax.ShapeDtypeStruct((STEPS, N), F32),
-        ],
-        in_specs=[pl.BlockSpec(memory_space=pltpu.VMEM)] * 2,
-        out_specs=[pl.BlockSpec(memory_space=pltpu.VMEM)] * 4,
-        scratch_shapes=[pltpu.VMEM((8, N), F32)],
-        compiler_params=pltpu.CompilerParams(vmem_limit_bytes=24 << 20),
-        name="reduced",
-    )(total, step_index.reshape(1, N))
-
-
-def final_kernel(ch_ref, cl_ref, y_ref, f_ref, wh_ref, wl_ref, d_ref, basis_ref, res_ref, acc):
+    stack[:N, :] = project.T
+    stack[N:, :] = jnp.broadcast_to(load * (scale * STEP), (8, N))
+
+
+def finish_kernel(
+    x_ref, step_ref, f_ref, ch_ref, cl_ref, y_ref, basis_ref, c_ref, res_ref,
+    weight, inverse, stack, upper, now, states,
+):
     step = pl.program_id(0)
     groups = CHUNK // B
-    here = pl.ds(step * groups, groups)
-    hi = ch_ref[here].reshape(CHUNK, N)
-    lo = cl_ref[here].reshape(CHUNK, N)
-    wh = wh_ref[...]
-    out = jnp.dot(hi, wh, preferred_element_type=F32)
-    out += jnp.dot(lo, wh, preferred_element_type=F32)
-    out += jnp.dot(hi, wl_ref[...], preferred_element_type=F32)
-    basis_ref[...] = out
-    last = d_ref[2:3, :]
-    before = d_ref[1:2, :]
-    lane = lax.broadcasted_iota(jnp.int32, (B, B), 1)
-    for g in range(CHUNK // B):
-        own = pl.ds(pl.multiple_of(step * CHUNK + g * B, B), B)
-        s = ch_ref[step * groups + g].astype(F32) + cl_ref[step * groups + g].astype(F32)
-        z = y_ref[own, :] * last - s * before
-        z = jnp.sum(z[:, :B] + z[:, B:], axis=1, keepdims=True)
-        acc[...] = jnp.where(lane == g, z, acc[...])
-    res_ref[...] = acc[...].T[: CHUNK // B, :] - STEP * f_ref[...]
-
-
-def final(cand_h, cand_l, y, forcing, wh, wl, d):
+
+    def basis():
+        here = pl.ds((step - 1) * groups, groups)
+        hi = ch_ref[here].reshape(CHUNK, N)
+        lo = cl_ref[here].reshape(CHUNK, N)
+        basis_ref[...] = jnp.dot(jnp.concatenate([hi, lo, hi], axis=1), weight[...], preferred_element_type=F32)
+
+    def half_turn():
+        stack[...] = dotf(stack[...], inverse[...], (1, 1))
+
+    def turn():
+        stack[...] = dotf(stack[...], inverse[...], (1, 0))
+        index = step_ref[...]
+        lane = lax.broadcasted_iota(jnp.int32, (1, N), 1)
+        latest = jnp.sum(jnp.where(index == jnp.max(index, axis=1, keepdims=True), lane, 0), axis=1, keepdims=True)
+        chosen = lax.broadcasted_iota(jnp.int32, (N, N), 0) == latest
+        now[...] = jnp.sum(jnp.where(chosen, stack[:N, :], 0.0), axis=0, keepdims=True) + stack[N:, :]
+        states[...] = jnp.zeros((8, N), F32)
+        states[0:1, :] = now[:1, :]
+
+    def advance(i):
+        now[...] = row_dot(now[...], split3(stack[:N, :]), (1, 0)) + stack[N:, :]
+        states[i : i + 1, :] = now[:1, :]
+
+    def coefficients():
+        c_ref[...] = row_dot(states[...], split3(upper[...]), (1, 1))[:STEPS, :]
+
+    def residual(*chunks):
+        last = states[2:3, :]
+        before = states[1:2, :]
+        lane = lax.broadcasted_iota(jnp.int32, (B, B), 1)
+        for chunk in chunks:
+            columns = jnp.zeros((B, B), F32)
+            for g in range(groups):
+                at = chunk * groups + g
+                s = ch_ref[at].astype(F32) + cl_ref[at].astype(F32)
+                z = y_ref[at * B : (at + 1) * B, :] * last - s * before
+                z = jnp.sum(z[:, :B] + z[:, B:], axis=1, keepdims=True)
+                columns = jnp.where(lane == g, z, columns)
+            rows = slice(chunk * groups, (chunk + 1) * groups)
+            res_ref[rows, :] = columns.T[:groups, :] - STEP * f_ref[rows, :]
+
+    def last_piece(k):
+        if k == 5:
+            coefficients()
+        residual(2 * (k - 5), 2 * (k - 5) + 1)
+
+    pieces = [half_turn, turn, functools.partial(advance, 1), functools.partial(advance, 2)]
+    pieces += [functools.partial(last_piece, k) for k in (5, 6, 7, 8)]
+
+    @pl.when(step == 0)
+    def _():
+        factor_step(x_ref, weight, inverse, stack, upper)
+
+    for k, piece in enumerate(pieces):
+
+        @pl.when(step == k + 1)
+        def _(piece=piece):
+            basis()
+            piece()
+
+
+def finish(total, step_index, forcing, cand_h, cand_l, y):
     rows = y.shape[0]
-    whole = lambda i: (0, 0)
+    whole = pl.BlockSpec(memory_space=pltpu.VMEM)
     return pl.pallas_call(
-        final_kernel,
-        grid=(rows // CHUNK,),
-        in_specs=[pl.BlockSpec(memory_space=pltpu.VMEM)] * 3
-        + [
-            pl.BlockSpec((CHUNK // B, B), lambda i: (i, 0)),
-            pl.BlockSpec((N, N), whole),
-            pl.BlockSpec((N, N), whole),
-            pl.BlockSpec((8, N), whole),
-        ],
-        out_specs=[
-            pl.BlockSpec((CHUNK, N), lambda i: (i, 0)),
-            pl.BlockSpec((CHUNK // B, B), lambda i: (i, 0)),
-        ],
+        finish_kernel,
+        grid=(rows // CHUNK + 1,),
+        in_specs=[whole] * 6,
+        out_specs=[pl.BlockSpec((CHUNK, N), lambda i: (jnp.maximum(i - 1, 0), 0)), whole, whole],
         out_shape=[
             jax.ShapeDtypeStruct((rows, N), F32),
+            jax.ShapeDtypeStruct((STEPS, N), F32),
             jax.ShapeDtypeStruct((rows // B, B), F32),
         ],
-        scratch_shapes=[pltpu.VMEM((B, B), F32)],
+        scratch_shapes=[
+            pltpu.VMEM((3 * N, N), BF16),
+            pltpu.VMEM((N, N), F32),
+            pltpu.VMEM((N + 8, N), F32),
+            pltpu.VMEM((N, N), F32),
+            pltpu.VMEM((8, N), F32),
+            pltpu.VMEM((8, N), F32),
+        ],
         compiler_params=pltpu.CompilerParams(vmem_limit_bytes=28 << 20),
-        cost_estimate=pl.CostEstimate(flops=6 * rows * N * N, bytes_accessed=12 * rows * N, transcendentals=0),
-        name="final",
-    )(cand_h, cand_l, y, forcing, wh, wl, d)
+        cost_estimate=pl.CostEstimate(flops=6 * rows * N * N, bytes_accessed=4 * rows * N, transcendentals=0),
+        name="finish",
+    )(total, step_index.reshape(1, N), forcing, cand_h, cand_l, y)
 
 
 def shards(snapshots, tangent, pattern, forcing, step_index):
     rows = snapshots.shape[0]
     blocks = rows // B
-    codes = pattern.T
-    source = codes // blocks
-    block = codes % blocks
-    tail_side = (source == 1) | (source == 3)
-    index_map = jnp.where(
-        source == 0, block, blocks + HALO * (source - 1) + block - jnp.where(tail_side, blocks - HALO, 0)
-    )
     cand_h, cand_l, gram_local = front(snapshots)
     force = forcing.reshape(blocks, B)
-    y, total = image(index_map, tangent, force, gram_local, cand_h, cand_l)
-    wh, wl, d, coefficients = reduced(total, step_index)
-    basis, residual = final(cand_h, cand_l, y, force, wh, wl, d)
+    y, total = image(pattern.T, tangent, force, gram_local, cand_h, cand_l)
+    basis, coefficients, residual = finish(total, step_index, force, cand_h, cand_l, y)
     return basis, coefficients, residual.reshape(rows)
 
 

time: 75 us -> 73.2 us (0.976)
  Pallas kernels: 73.4 us -> 72.4 us
    pallas_call x2 -> x1, Pallas kernels: 17.5 us -> 16.6 us  [finish(): pl.pallas_call(finish_kernel, grid=(rows // CHUNK + 1,), in_specs=[whole]...]
where the time goes in v5:
time: 73.2 us; the launch traced here: 73.1 us
  Pallas kernels  72.4 us (99%)
    pallas_call x1, Pallas kernels, image(): pl.pallas_call(image_kernel, grid_spec=pltpu.PrefetchScalarGridSpec(num_s...  35.3 us
    pallas_call x1, Pallas kernels, front(): pl.pallas_call(front_kernel, in_specs=[pl.BlockSpec(memory_space=pl.ANY)]...  20.6 us
    pallas_call x1, Pallas kernels, finish(): pl.pallas_call(finish_kernel, grid=(rows // CHUNK + 1,), in_specs=[whole]...  16.6 us

profile of v5, /device:TPU:1, one launch (start us, length us, event | category | flops | bytes accessed | tf_op | source)
XLA Modules:
  0.0 73.1 jit_solution(2736744198279620686)
XLA Ops:
  0.6 0.0 copy-start
  0.6 0.0 copy-start.2
  0.7 20.6 %front.1 = (bf16[80,128,256]{2,1,0:T(8,128)(2,1)S(1)}, bf16[80,128,256]{2,1,0:T(8,128)(2,1)S(1)}, f32[256,256]{1,0:T(8,128)S(1)}) custom-call(f32[8192,256]{1,0:T(8,128)} %s_hbm.1), custom_call_target="tpu_custom_call" | custom-call | flops 1073741824 | bytes 16777216 | tf_op jit(solution)/shard_map/front/pallas_call | solution.py:91
  21.2 0.0 copy-done
  21.2 0.0 copy-done.2
  21.2 0.0 copy-start.1
  21.2 35.3 %image.1 = (f32[8192,256]{1,0:T(8,128)S(1)}, f32[1344,128]{1,0:T(8,128)S(1)}) custom-call(s32[4,64]{1,0:T(4,128)S(1)} %bitcast.7, bf16[8192,512]{1,0:T(8,128)(2,1)} %t_ref.1, f32[64,128]{1,0:T(8,128)S(1)} %bitcast.4, f32[256,256]{1,0:T(8,128)S(1)} %get-tuple-element.11.g_ref, bf16[80,128,256]{2,1,0:T(8,128)(2,1)S(1)} %get-tuple-element.12.cand_h.ch_ref, ...), custom_call_target="tpu_custom_call" | custom-call | flops 10737418240 | bytes 16777216 | tf_op jit(solution)/shard_map/image/pallas_call | solution.py:266
  56.5 0.0 copy-done.1
  56.5 16.6 %finish.1 = (f32[8192,256]{1,0:T(8,128)}, f32[3,256]{1,0:T(4,128)}, f32[64,128]{1,0:T(8,128)}) custom-call(f32[1344,128]{1,0:T(8,128)S(1)} %get-tuple-element.14.x_ref, s32[1,256]{1,0:T(1,128)S(1)} %bitcast.6, f32[64,128]{1,0:T(8,128)S(1)} %bitcast.5, bf16[80,128,256]{2,1,0:T(8,128)(2,1)S(1)} %get-tuple-element.12.cand_h.ch_ref, ...), custom_call_target="tpu_custom_call" | custom-call | flops 3221225472 | bytes 8388608 | tf_op jit(solution)/shard_map/finish/pallas_call | solution.py:492
Async XLA Ops:
  0.6 20.6 %copy-start = (f32[8192]{0:T(1024)S(1)}, f32[8192]{0:T(1024)}, u32[]{:S(2)}) copy-start(f32[8192]{0:T(1024)} %param.8) | copy-start | bytes 98308
  0.6 20.6 %copy-start.2 = (s32[64,4]{0,1:T(4,128)S(1)}, s32[64,4]{0,1:T(4,128)}, u32[]{:S(2)}) copy-start(s32[64,4]{0,1:T(4,128)} %param.7) | copy-start | bytes 3076
  21.2 35.3 %copy-start.1 = (s32[256]{0:T(256)S(1)}, s32[256]{0:T(256)}, u32[]{:S(2)}) copy-start(s32[256]{0:T(256)} %param.9) | copy-start | bytes 3076

commit v6 on v5

--- a/solution.py
+++ b/solution.py
@@ -13,6 +13,7 @@
 B = 128
 N = 256
 CHUNK = 1024
+SPAN = 2048
 PACK = 1344
 F32 = jnp.float32
 BF16 = jnp.bfloat16
@@ -426,9 +427,9 @@
     groups = CHUNK // B
 
     def basis():
-        here = pl.ds((step - 1) * groups, groups)
-        hi = ch_ref[here].reshape(CHUNK, N)
-        lo = cl_ref[here].reshape(CHUNK, N)
+        here = pl.ds((step - 1) * (SPAN // B), SPAN // B)
+        hi = ch_ref[here].reshape(SPAN, N)
+        lo = cl_ref[here].reshape(SPAN, N)
         basis_ref[...] = jnp.dot(jnp.concatenate([hi, lo, hi], axis=1), weight[...], preferred_element_type=F32)
 
     def half_turn():
@@ -466,13 +467,19 @@
             rows = slice(chunk * groups, (chunk + 1) * groups)
             res_ref[rows, :] = columns.T[:groups, :] - STEP * f_ref[rows, :]
 
-    def last_piece(k):
-        if k == 5:
-            coefficients()
-        residual(2 * (k - 5), 2 * (k - 5) + 1)
-
-    pieces = [half_turn, turn, functools.partial(advance, 1), functools.partial(advance, 2)]
-    pieces += [functools.partial(last_piece, k) for k in (5, 6, 7, 8)]
+    def start():
+        half_turn()
+        turn()
+
+    def march():
+        for i in range(1, STEPS):
+            advance(i)
+
+    def first_half():
+        residual(0, 1, 2, 3)
+        coefficients()
+
+    pieces = [start, march, first_half, functools.partial(residual, 4, 5, 6, 7)]
 
     @pl.when(step == 0)
     def _():
@@ -491,9 +498,9 @@
     whole = pl.BlockSpec(memory_space=pltpu.VMEM)
     return pl.pallas_call(
         finish_kernel,
-        grid=(rows // CHUNK + 1,),
+        grid=(rows // SPAN + 1,),
         in_specs=[whole] * 6,
-        out_specs=[pl.BlockSpec((CHUNK, N), lambda i: (jnp.maximum(i - 1, 0), 0)), whole, whole],
+        out_specs=[pl.BlockSpec((SPAN, N), lambda i: (jnp.maximum(i - 1, 0), 0)), whole, whole],
         out_shape=[
             jax.ShapeDtypeStruct((rows, N), F32),
             jax.ShapeDtypeStruct((STEPS, N), F32),

time: 73.2 us -> 72.9 us (level)
  no operation moved by 1% of the time
where the time goes in v6:
time: 72.9 us; the launch traced here: 72.8 us
  Pallas kernels  72.1 us (99%)
    pallas_call x1, Pallas kernels, image(): pl.pallas_call(image_kernel, grid_spec=pltpu.PrefetchScalarGridSpec(num_s...  35.3 us
    pallas_call x1, Pallas kernels, front(): pl.pallas_call(front_kernel, in_specs=[pl.BlockSpec(memory_space=pl.ANY)]...  20.6 us
    pallas_call x1, Pallas kernels, finish(): pl.pallas_call(finish_kernel, grid=(rows // SPAN + 1,), in_specs=[whole]...  16.3 us

profile of v6, /device:TPU:1, one launch (start us, length us, event | category | flops | bytes accessed | tf_op | source)
XLA Modules:
  0.0 72.8 jit_solution(10809626790895744309)
XLA Ops:
  0.6 0.0 copy-start
  0.6 0.0 copy-start.2
  0.7 20.6 %front.1 = (bf16[80,128,256]{2,1,0:T(8,128)(2,1)S(1)}, bf16[80,128,256]{2,1,0:T(8,128)(2,1)S(1)}, f32[256,256]{1,0:T(8,128)S(1)}) custom-call(f32[8192,256]{1,0:T(8,128)} %s_hbm.1), custom_call_target="tpu_custom_call" | custom-call | flops 1073741824 | bytes 16777216 | tf_op jit(solution)/shard_map/front/pallas_call | solution.py:92
  21.2 0.0 copy-done
  21.2 0.0 copy-done.2
  21.2 0.0 copy-start.1
  21.2 35.3 %image.1 = (f32[8192,256]{1,0:T(8,128)S(1)}, f32[1344,128]{1,0:T(8,128)S(1)}) custom-call(s32[4,64]{1,0:T(4,128)S(1)} %bitcast.7, bf16[8192,512]{1,0:T(8,128)(2,1)} %t_ref.1, f32[64,128]{1,0:T(8,128)S(1)} %bitcast.4, f32[256,256]{1,0:T(8,128)S(1)} %get-tuple-element.11.g_ref, bf16[80,128,256]{2,1,0:T(8,128)(2,1)S(1)} %get-tuple-element.12.cand_h.ch_ref, ...), custom_call_target="tpu_custom_call" | custom-call | flops 10737418240 | bytes 16777216 | tf_op jit(solution)/shard_map/image/pallas_call | solution.py:267
  56.5 0.0 copy-done.1
  56.5 16.3 %finish.1 = (f32[8192,256]{1,0:T(8,128)}, f32[3,256]{1,0:T(4,128)}, f32[64,128]{1,0:T(8,128)}) custom-call(f32[1344,128]{1,0:T(8,128)S(1)} %get-tuple-element.14.x_ref, s32[1,256]{1,0:T(1,128)S(1)} %bitcast.6, f32[64,128]{1,0:T(8,128)S(1)} %bitcast.5, bf16[80,128,256]{2,1,0:T(8,128)(2,1)S(1)} %get-tuple-element.12.cand_h.ch_ref, ...), custom_call_target="tpu_custom_call" | custom-call | flops 3221225472 | bytes 8388608 | tf_op jit(solution)/shard_map/finish/pallas_call | solution.py:499
Async XLA Ops:
  0.6 20.6 %copy-start = (f32[8192]{0:T(1024)S(1)}, f32[8192]{0:T(1024)}, u32[]{:S(2)}) copy-start(f32[8192]{0:T(1024)} %param.8) | copy-start | bytes 98308
  0.6 20.6 %copy-start.2 = (s32[64,4]{0,1:T(4,128)S(1)}, s32[64,4]{0,1:T(4,128)}, u32[]{:S(2)}) copy-start(s32[64,4]{0,1:T(4,128)} %param.7) | copy-start | bytes 3076
  21.2 35.3 %copy-start.1 = (s32[256]{0:T(256)S(1)}, s32[256]{0:T(256)}, u32[]{:S(2)}) copy-start(s32[256]{0:T(256)} %param.9) | copy-start | bytes 3076

commit v7 on v6

--- a/solution.py
+++ b/solution.py
@@ -166,26 +166,26 @@
     for p, (a, b, c) in enumerate(orders):
         arrive(0, p)
         acc[p] = x_ref[pl.ds(p * PART + mine, half), :] + got0[p]
-        for o in (1, 2, 3):
+        for o in (2, 1, 3):
             there = (place[a] + o) % 4
             send(1, p, o - 1, acc.at[p, pl.ds(there * quarter, quarter)], got1.at[p, o - 1], a, o)
     for p, (a, b, c) in enumerate(orders):
         arrive(1, p)
         slot = got2.at[p, place[b]]
         slot[...] = acc[p, pl.ds(place[a] * quarter, quarter), :] + got1[p, 0] + got1[p, 1] + got1[p, 2]
-        for o in (1, 2, 3):
+        for o in (2, 1, 3):
             send(2, p, o - 1, slot, slot, b, o)
     for p, (a, b, c) in enumerate(orders):
         arrive(2, p)
         slot = got3.at[p, place[c]]
         slot[...] = got2[p, 0] + got2[p, 1] + got2[p, 2] + got2[p, 3]
-        for o in (1, 2, 3):
+        for o in (2, 1, 3):
             send(3, p, o - 1, slot, slot, c, o)
     for p, (a, b, c) in enumerate(orders):
         arrive(3, p)
         spot = o_ref.at[pl.ds(p * PART + mine + place[a] * quarter, quarter)]
         spot[...] = got3[p, 0] + got3[p, 1] + got3[p, 2] + got3[p, 3]
-        for o in (1, 2, 3):
+        for o in (2, 1, 3):
             send(4, p, o - 1, spot, spot, a, o)
     for p in range(PARTS):
         arrive(4, p)

time: 72.9 us -> 72.3 us (level)
  no operation moved by 1% of the time
where the time goes in v7:
time: 72.3 us; the launch traced here: 72.2 us
  Pallas kernels  71.5 us (99%)
    pallas_call x1, Pallas kernels, image(): pl.pallas_call(image_kernel, grid_spec=pltpu.PrefetchScalarGridSpec(num_s...  34.6 us
    pallas_call x1, Pallas kernels, front(): pl.pallas_call(front_kernel, in_specs=[pl.BlockSpec(memory_space=pl.ANY)]...  20.6 us
    pallas_call x1, Pallas kernels, finish(): pl.pallas_call(finish_kernel, grid=(rows // SPAN + 1,), in_specs=[whole]...  16.3 us

profile of v7, /device:TPU:1, one launch (start us, length us, event | category | flops | bytes accessed | tf_op | source)
XLA Modules:
  0.0 72.2 jit_solution(8337114323452019242)
XLA Ops:
  0.6 0.0 copy-start
  0.6 0.0 copy-start.2
  0.7 20.6 %front.1 = (bf16[80,128,256]{2,1,0:T(8,128)(2,1)S(1)}, bf16[80,128,256]{2,1,0:T(8,128)(2,1)S(1)}, f32[256,256]{1,0:T(8,128)S(1)}) custom-call(f32[8192,256]{1,0:T(8,128)} %s_hbm.1), custom_call_target="tpu_custom_call" | custom-call | flops 1073741824 | bytes 16777216 | tf_op jit(solution)/shard_map/front/pallas_call | solution.py:92
  21.2 0.0 copy-done
  21.2 0.0 copy-done.2
  21.2 0.0 copy-start.1
  21.2 34.6 %image.1 = (f32[8192,256]{1,0:T(8,128)S(1)}, f32[1344,128]{1,0:T(8,128)S(1)}) custom-call(s32[4,64]{1,0:T(4,128)S(1)} %bitcast.7, bf16[8192,512]{1,0:T(8,128)(2,1)} %t_ref.1, f32[64,128]{1,0:T(8,128)S(1)} %bitcast.4, f32[256,256]{1,0:T(8,128)S(1)} %get-tuple-element.11.g_ref, bf16[80,128,256]{2,1,0:T(8,128)(2,1)S(1)} %get-tuple-element.12.cand_h.ch_ref, ...), custom_call_target="tpu_custom_call" | custom-call | flops 10737418240 | bytes 16777216 | tf_op jit(solution)/shard_map/image/pallas_call | solution.py:267
  55.9 0.0 copy-done.1
  55.9 16.3 %finish.1 = (f32[8192,256]{1,0:T(8,128)}, f32[3,256]{1,0:T(4,128)}, f32[64,128]{1,0:T(8,128)}) custom-call(f32[1344,128]{1,0:T(8,128)S(1)} %get-tuple-element.14.x_ref, s32[1,256]{1,0:T(1,128)S(1)} %bitcast.6, f32[64,128]{1,0:T(8,128)S(1)} %bitcast.5, bf16[80,128,256]{2,1,0:T(8,128)(2,1)S(1)} %get-tuple-element.12.cand_h.ch_ref, ...), custom_call_target="tpu_custom_call" | custom-call | flops 3221225472 | bytes 8388608 | tf_op jit(solution)/shard_map/finish/pallas_call | solution.py:499
Async XLA Ops:
  0.6 20.6 %copy-start = (f32[8192]{0:T(1024)S(1)}, f32[8192]{0:T(1024)}, u32[]{:S(2)}) copy-start(f32[8192]{0:T(1024)} %param.8) | copy-start | bytes 98308
  0.6 20.6 %copy-start.2 = (s32[64,4]{0,1:T(4,128)S(1)}, s32[64,4]{0,1:T(4,128)}, u32[]{:S(2)}) copy-start(s32[64,4]{0,1:T(4,128)} %param.7) | copy-start | bytes 3076
  21.2 34.7 %copy-start.1 = (s32[256]{0:T(256)S(1)}, s32[256]{0:T(256)}, u32[]{:S(2)}) copy-start(s32[256]{0:T(256)} %param.9) | copy-start | bytes 3076
